TPU v7x, 512 devices: a whole 4x8x8 slice. The times are simulated.
512 devices in a mesh: cells: 128 (over z, y_lo, x, core), stations: 4 (over y_hi).
Axes of the slice: x: 4, y: 8 (y_hi: 4, y_lo: 2; y = y_hi * 2 + y_lo), z: 8, core: 2. Of those that a mesh axis runs over, the one named last changes fastest.
Arguments:
- probes: bfloat16 [16, 524288], P(None, 'cells'), may hold values from -6 to 6
- reg_weight: float32 [524288], P('cells'), may hold values from 0.1 to 1
- cell_plan: int32 [2, 524288], P(None, 'cells'), may hold values from 0 to 255
- cell_depth: int32 [524288], P('cells'), may hold values from 0 to 15, as said below
- station_index: int32 [2, 16384], P(None, 'stations'), may hold values from 0 to 65535, as said below
- station_weight: float32 [16384], P('stations'), may hold values from 0.5 to 2
Outputs:
- basis: float32 [16, 524288], P(None, ('cells', 'stations'))
- factor: float32 [16, 16], replicated
Inputs may be any that keep to these rules, and one draw needn't show every extreme that they name: `cell_plan`: east and north cell indices of a grid of 256 by 256 columns. `cell_depth`: depth indices of 16 layers. `station_index`: east and north station positions in 1/256ths of a cell width, over the same area as the cells' grid.
All inputs are finite; a program needn't handle non-finite values.
Results may differ from a plain program's by a relative error of at most 0.00065.
Values may be sent and summed in bfloat16 or wider, within the bound.
No kernel may reach another device: no remote copies, remote signals or barrier semaphores. Data moves between devices by JAX's collectives and lax.ppermute only.
A program may use at most 64 MiB of HBM per device.

v0:
```python
import math

import jax
import jax.numpy as jnp
from jax import lax
from jax.sharding import PartitionSpec as P

GRAVITY = 2.0
JITTER = 1e-06
SUBSTEP = 0.00390625


def cell_points(cell_plan, cell_depth):
    cell_east = cell_plan[0].astype(jnp.float32) + 0.5
    cell_north = cell_plan[1].astype(jnp.float32) + 0.5
    cell_down = cell_depth.astype(jnp.float32) + 1.0
    return (cell_east, cell_north, cell_down)


def sensitivity(st_east, st_north, cell_geom):
    cell_east, cell_north, cell_down = cell_geom
    d_east = cell_east[None, :] - st_east[:, None]
    d_north = cell_north[None, :] - st_north[:, None]
    distance = d_east * d_east + d_north * d_north + cell_down[None, :] * cell_down[None, :]
    inverse = lax.rsqrt(distance)
    return (GRAVITY * cell_down[None, :] * inverse * inverse * inverse).astype(jnp.bfloat16)


def forward_terms(probes, st_east, st_north, cell_geom):
    station_count = st_east.shape[0]
    block_size = math.gcd(station_count, 512)

    def forward_advance(turn_index, running):
        start_at = turn_index * block_size
        sens_tile = sensitivity(
            lax.dynamic_slice_in_dim(st_east, start_at, block_size),
            lax.dynamic_slice_in_dim(st_north, start_at, block_size),
            cell_geom,
        )
        partial_value = lax.dot_general(
            probes, sens_tile, (((1,), (1,)), ((), ())), preferred_element_type=jnp.float32
        )
        return lax.dynamic_update_slice_in_dim(running, partial_value, start_at, 1)

    zero_field = jnp.zeros((probes.shape[0], station_count), jnp.float32)
    return lax.fori_loop(0, station_count // block_size, forward_advance, zero_field)


def transposed_add(running, weighted, st_east, st_north, cell_geom):
    station_count = weighted.shape[1]
    block_size = math.gcd(station_count, 512)

    def transposed_advance(turn_index, current):
        start_at = turn_index * block_size
        sens_tile = sensitivity(
            lax.dynamic_slice_in_dim(st_east, start_at, block_size),
            lax.dynamic_slice_in_dim(st_north, start_at, block_size),
            cell_geom,
        )
        segment = lax.dynamic_slice_in_dim(weighted, start_at, block_size, 1)
        return current + jnp.dot(segment, sens_tile, preferred_element_type=jnp.float32)

    return lax.fori_loop(0, station_count // block_size, transposed_advance, running)


def gram_term(hess_image):
    return jnp.dot(
        hess_image,
        hess_image.T,
        precision=lax.Precision.HIGHEST,
        preferred_element_type=jnp.float32,
    )


def body(probes, reg_weight, cell_plan, cell_depth, station_index, station_weight):
    cell_geom = cell_points(cell_plan, cell_depth)
    st_east = station_index[0].astype(jnp.float32) * SUBSTEP
    st_north = station_index[1].astype(jnp.float32) * SUBSTEP
    station_scale = station_weight * station_weight
    terms = forward_terms(probes, st_east, st_north, cell_geom)
    zero_image = jnp.zeros((probes.shape[0], probes.shape[1]), jnp.float32)
    station_field = lax.psum(terms, "cells")
    weighted = (station_scale[None, :] * station_field).astype(jnp.bfloat16)
    backward = transposed_add(zero_image, weighted, st_east, st_north, cell_geom)
    group_count = lax.axis_size("stations")
    quarter = probes.shape[1] // group_count
    offset_cells = lax.axis_index("stations") * quarter
    cell_total = probes.shape[1] * lax.axis_size("cells")
    summed = lax.psum(backward, "stations")
    hess_image = summed + reg_weight[None, :] * probes.astype(jnp.float32)
    gram_matrix = lax.psum(gram_term(hess_image), "cells")
    local_image = lax.dynamic_slice_in_dim(hess_image, offset_cells, quarter, 1)
    gram_matrix = gram_matrix / cell_total + JITTER * jnp.eye(probes.shape[0], dtype=jnp.float32)
    lower_factor = jnp.linalg.cholesky(gram_matrix)
    basis_rows = jax.scipy.linalg.solve_triangular(lower_factor, local_image, lower=True)
    return (basis_rows, lower_factor)


def solution(mesh):
    return jax.shard_map(
        body,
        mesh=mesh,
        in_specs=(
            P(None, "cells"),
            P("cells"),
            P(None, "cells"),
            P("cells"),
            P(None, "stations"),
            P("stations"),
        ),
        out_specs=(P(None, ("cells", "stations")), P()),
        check_vma=False,
    )
```

profile of v0, /device:TPU:1, one launch (start us, length us, event | category | flops | bytes accessed | tf_op | source)
XLA Modules:
  0.0 1376.9 jit_solution(104188721798137522)
XLA Ops:
  7.2 0.9 convert_add_fusion
  8.1 0.9 convert_multiply_fusion
  9.0 0.7 fusion.23
  9.7 25.5 %while.29 = (s32[]{:T(128)}, f32[16,4096]{1,0:T(8,128)S(1)}, f32[4096]{0:T(1024)S(1)}, f32[4096]{0:T(1024)S(1)}, f32[4096]{0:T(1024)S(1)}, /*index=5*/f32[4096]{...) while((s32[]{:T(128)}, f32[16,4096]{1,0:T(8,128)S(1)}, ...), condition=%wide.region_1.0_spmd, body=%wide.region_0.0_spmd.sunk | while | flops 88084488 | bytes 274615 | solution.py:46
  9.7 0.1 dynamic_slice.56
  9.9 3.0 fusion.35
  12.9 0.1 dynamic_slice.56
  13.0 0.1 dynamic_slice.57
  13.1 3.0 fusion.35
  16.3 3.0 fusion.35
  19.4 0.1 dynamic_slice.57
  19.5 3.0 fusion.35
  22.5 0.1 dynamic_slice.56
  22.6 0.1 dynamic_slice.57
  22.6 3.0 fusion.35
  25.8 3.0 fusion.35
  29.0 3.0 fusion.35
  32.2 3.0 fusion.35
  35.2 0.7 copy-done
  36.1 966.6 %all-reduce.3.cloned.1.call-done = f32[16,4096]{1,0:T(8,128)} async-done(((f32[16,4096]{1,0:T(8,128)}), f32[16,4096]{1,0:T(8,128)}) %all-reduce.3.cloned.1.call-update) | async-done | bytes 262160 | tf_op jit(solution)/shard_map/psum | solution.py:82
  1002.6 1.0 multiply_convert_fusion
  1003.6 25.6 %while.30 = (s32[]{:T(128)}, f32[16,4096]{1,0:T(8,128)S(1)}, bf16[16,4096]{1,0:T(8,128)(2,1)S(1)}, f32[4096]{0:T(1024)S(1)}, f32[4096]{0:T(1024)S(1)}, /*index=5...) while((s32[]{:T(128)}, f32[16,4096]{1,0:T(8,128)S(1)}, ...), condition=%wide.region_4.0_spmd.clone, body=%wide.region_3.0_spmd.clone.sunk | while | flops 88215560 | bytes 651457 | solution.py:63
  1003.6 0.1 dynamic_slice.59
  1003.8 3.0 convolution_add_fusion.2
  1006.8 0.1 dynamic_slice.59
  1007.0 3.0 convolution_add_fusion.2
  1010.0 0.1 dynamic_slice.59
  1010.2 3.0 convolution_add_fusion.2
  1013.2 0.1 dynamic_slice.59
  1013.4 3.0 convolution_add_fusion.2
  1016.4 0.1 dynamic_slice.59
  1016.6 3.0 convolution_add_fusion.2
  1019.6 0.1 dynamic_slice.59
  1019.8 3.0 convolution_add_fusion.2
  1022.8 0.1 dynamic_slice.59
  1023.0 3.0 convolution_add_fusion.2
  1026.0 0.1 dynamic_slice.59
  1026.2 3.0 convolution_add_fusion.2
  1029.3 0.7 copy-done.1
  1030.0 50.5 %all-reduce.5.cloned.1.call-done = f32[16,4096]{1,0:T(8,128)} async-done(((f32[16,4096]{1,0:T(8,128)}), f32[16,4096]{1,0:T(8,128)}) %all-reduce.5.cloned.1.call-update) | async-done | bytes 262160 | tf_op jit(solution)/shard_map/psum | solution.py:89
  1080.5 1.0 multiply_add_fusion
  1081.5 0.5 fusion.24
  1082.0 282.5 %psum.23 = f32[16,16]{1,0:T(8,128)S(1)} all-reduce(f32[16,16]{1,0:T(8,128)S(1)} %fusion.24), channel_id=1, replica_groups=mesh['cells'=128,'stations'=4] {'cells'}, use_global_device_ids=true, to_apply=%region_6.0 | all-reduce | flops 256 | bytes 2048 | tf_op jit(solution)/shard_map/psum | solution.py:91
  1364.6 1.5 cholesky.16
  1366.1 0.6 compare_reduce_fusion
  1366.7 1.2 select_bitcast_fusion
  1368.0 1.2 custom-call.7
  1369.2 0.9 fusion.18
  (53 shorter events, 1.7 us)
Async XLA Ops:
  7.2 2.6 copy-start.2
  7.2 995.5 %all-reduce.3.cloned.1.call-start = ((), (), s32[]{:S(2)}) async-start(), calls=%async_computation | async-start | bytes 524288 | tf_op jit(solution)/shard_map/psum | solution.py:82
  35.2 0.7 copy-start
  35.2 0.8 copy-start.3
  36.0 1044.5 %all-reduce.5.cloned.1.call-start = ((), (), s32[]{:S(2)}) async-start(), calls=%async_computation.1 | async-start | bytes 524288 | tf_op jit(solution)/shard_map/psum | solution.py:89
  1029.2 0.7 copy-start.1
  1029.2 51.3 %copy-start.4 = (f32[4096]{0:T(1024)S(1)}, f32[4096]{0:T(1024)}, u32[]{:S(2)}) copy-start(f32[4096]{0:T(1024)} %param.11) | copy-start | bytes 49156
Sparse Core Ops, SparseCore 0:
  36.1 966.4 all-reduce.2
  1030.1 50.3 all-reduce.4
where the time goes:
time: 1380 us
  waiting for transfers between devices  1020 us (74%)
  blocking collectives  283 us (21%)
  matrix products  50 us (4%)
  between operations  14.1 us (1%)
    psum x1, waiting for transfers between devices, body(): station_field = lax.psum(terms, 'cells')  967 us
    psum x1, blocking collectives, body(): gram_matrix = lax.psum(gram_term(hess_image), 'cells')  283 us
    psum x1, waiting for transfers between devices, body(): summed = lax.psum(backward, 'stations')  50.5 us
  transfers between devices with their start and end apart: 2, of which 2 were waited for; matrix products, arithmetic and copies ran while one was open for 0% of the time, Pallas kernels for 0%

commit v1 on v0

--- a/solution.py
+++ b/solution.py
@@ -3,11 +3,14 @@
 import jax
 import jax.numpy as jnp
 from jax import lax
-from jax.sharding import PartitionSpec as P
+from jax.sharding import Mesh, PartitionSpec as P
 
 GRAVITY = 2.0
 JITTER = 1e-06
 SUBSTEP = 0.00390625
+CELL_AXES = ("z", "yl", "x", "c")
+NEAR = ("x", "c", "yh")
+FAR = ("z", "yl")
 
 
 def cell_points(cell_plan, cell_depth):
@@ -72,24 +75,42 @@
     )
 
 
+def exchanged(blocks, axes):
+    return lax.all_to_all(blocks, axes, 0, 0, tiled=True)
+
+
+def group_sum(value, axes):
+    copies = jnp.broadcast_to(value[None], (lax.axis_size(axes), *value.shape))
+    return jnp.sum(exchanged(copies, axes), axis=0)
+
+
 def body(probes, reg_weight, cell_plan, cell_depth, station_index, station_weight):
     cell_geom = cell_points(cell_plan, cell_depth)
     st_east = station_index[0].astype(jnp.float32) * SUBSTEP
     st_north = station_index[1].astype(jnp.float32) * SUBSTEP
     station_scale = station_weight * station_weight
     terms = forward_terms(probes, st_east, st_north, cell_geom)
+    blocks = terms.reshape(2, 2, 4, 32, 128).transpose(0, 3, 1, 2, 4).reshape(128, 4, 128)
+    own_field = jnp.sum(exchanged(blocks, CELL_AXES), axis=0)
+    own_block = (lax.axis_index(CELL_AXES) % 64) // 2
+    own_scale = lax.dynamic_slice_in_dim(station_scale, own_block * 128, 128)
+    own_weighted = (own_scale[None, :] * own_field).astype(jnp.bfloat16)
+    gathered = exchanged(jnp.broadcast_to(own_weighted[None], (128, 4, 128)), CELL_AXES)
+    weighted = gathered.reshape(2, 32, 2, 4, 128).transpose(0, 2, 3, 1, 4).reshape(16, 4096)
     zero_image = jnp.zeros((probes.shape[0], probes.shape[1]), jnp.float32)
-    station_field = lax.psum(terms, "cells")
-    weighted = (station_scale[None, :] * station_field).astype(jnp.bfloat16)
     backward = transposed_add(zero_image, weighted, st_east, st_north, cell_geom)
-    group_count = lax.axis_size("stations")
+    group_count = lax.axis_size("yh")
     quarter = probes.shape[1] // group_count
-    offset_cells = lax.axis_index("stations") * quarter
-    cell_total = probes.shape[1] * lax.axis_size("cells")
-    summed = lax.psum(backward, "stations")
-    hess_image = summed + reg_weight[None, :] * probes.astype(jnp.float32)
-    gram_matrix = lax.psum(gram_term(hess_image), "cells")
-    local_image = lax.dynamic_slice_in_dim(hess_image, offset_cells, quarter, 1)
+    offset_cells = lax.axis_index("yh") * quarter
+    cell_total = probes.shape[1] * lax.axis_size(CELL_AXES)
+    parts = backward.reshape(16, group_count, quarter).transpose(1, 0, 2)
+    summed = jnp.sum(exchanged(parts, "yh"), axis=0)
+    own_reg = lax.dynamic_slice_in_dim(reg_weight, offset_cells, quarter)
+    own_probes = lax.dynamic_slice_in_dim(probes, offset_cells, quarter, 1)
+    local_image = summed + own_reg[None, :] * own_probes.astype(jnp.float32)
+    gram_flat = gram_term(local_image).reshape(2, 128)
+    gram_flat = group_sum(group_sum(gram_flat, NEAR), FAR)
+    gram_matrix = gram_flat.reshape(16, 16)
     gram_matrix = gram_matrix / cell_total + JITTER * jnp.eye(probes.shape[0], dtype=jnp.float32)
     lower_factor = jnp.linalg.cholesky(gram_matrix)
     basis_rows = jax.scipy.linalg.solve_triangular(lower_factor, local_image, lower=True)
@@ -97,17 +118,18 @@
 
 
 def solution(mesh):
+    split = Mesh(mesh.devices.reshape(8, 2, 4, 2, 4), ("z", "yl", "x", "c", "yh"))
     return jax.shard_map(
         body,
-        mesh=mesh,
+        mesh=split,
         in_specs=(
-            P(None, "cells"),
-            P("cells"),
-            P(None, "cells"),
-            P("cells"),
-            P(None, "stations"),
-            P("stations"),
+            P(None, CELL_AXES),
+            P(CELL_AXES),
+            P(None, CELL_AXES),
+            P(CELL_AXES),
+            P(None, "yh"),
+            P("yh"),
         ),
-        out_specs=(P(None, ("cells", "stations")), P()),
+        out_specs=(P(None, (*CELL_AXES, "yh")), P()),
         check_vma=False,
     )

time: 1380 us -> 152 us (0.11)
  waiting for transfers between devices: 1020 us -> 30.7 us
  blocking collectives: 283 us -> 26.6 us
  starting transfers between devices: 0.08 us -> 29.2 us
    psum x2 -> x0, waiting for transfers between devices: 1020 us -> none  [the longest x1 967 us: body(): station_field = lax.psum(terms, 'cells')]
    psum x1 -> x0, blocking collectives: 283 us -> none  [body(): gram_matrix = lax.psum(gram_term(hess_image), 'cells')]
    all_to_all x0 -> x3, waiting for transfers between devices: none -> 30.7 us  [exchanged(): return lax.all_to_all(blocks, axes, 0, 0, tiled=True)]
    all_to_all x0 -> x3, starting transfers between devices: none -> 29.2 us  [exchanged(): return lax.all_to_all(blocks, axes, 0, 0, tiled=True)]
    all_to_all x0 -> x2, blocking collectives: none -> 26.6 us  [exchanged(): return lax.all_to_all(blocks, axes, 0, 0, tiled=True)]
  transfers between devices with their start and end apart: 2 -> 3, of which waited for: 2 -> 3; matrix products, arithmetic and copies ran while one was open for 0% -> 1% of each run, Pallas kernels for 0% -> 0%
where the time goes in v1:
time: 152 us
  matrix products  49.7 us (33%)
  waiting for transfers between devices  30.7 us (20%)
  starting transfers between devices  29.2 us (19%)
  blocking collectives  26.6 us (18%)
  other arithmetic  8.16 us (5%)
  local copies, waits for them, and re-layouts  6.32 us (4%)
    all_to_all x3, waiting for transfers between devices, exchanged(): return lax.all_to_all(blocks, axes, 0, 0, tiled=True)  30.7 us
    all_to_all x3, starting transfers between devices, exchanged(): return lax.all_to_all(blocks, axes, 0, 0, tiled=True)  29.2 us
    all_to_all x2, blocking collectives, exchanged(): return lax.all_to_all(blocks, axes, 0, 0, tiled=True)  26.6 us
    dot_general x8, matrix products, transposed_advance(): jnp.dot(segment, sens_tile, preferred_element_type=jnp.float32)  24.4 us
    dot_general x8, matrix products, forward_advance(): lax.dot_general(probes, sens_tile, (((1,), (1,)), ((), ())), preferred_el...  24.3 us
  transfers between devices with their start and end apart: 3, of which 3 were waited for; matrix products, arithmetic and copies ran while one was open for 1% of the time, Pallas kernels for 0%

profile of v1, /device:TPU:1, one launch (start us, length us, event | category | flops | bytes accessed | tf_op | source)
XLA Modules:
  0.0 151.5 jit_solution(4770715829350580415)
XLA Ops:
  0.6 0.9 convert_add_fusion
  1.5 0.9 convert_multiply_fusion
  2.4 0.7 fusion.28
  3.1 25.5 %while.29 = (s32[]{:T(128)}, f32[16,4096]{1,0:T(8,128)S(1)}, f32[4096]{0:T(1024)S(1)}, f32[4096]{0:T(1024)S(1)}, f32[4096]{0:T(1024)S(1)}, /*index=5*/f32[4096]{...) while((s32[]{:T(128)}, f32[16,4096]{1,0:T(8,128)S(1)}, ...), condition=%wide.region_1.0_spmd, body=%wide.region_0.0_spmd.sunk | while | flops 88084488 | bytes 274615 | solution.py:49
  3.2 0.1 dynamic_slice.72
  3.3 3.0 %fusion.37 = f32[16,4096]{1,0:T(8,128)S(1)} fusion(f32[16,4096]{1,0:T(8,128)S(1)} %get-tuple-element.554, s32[]{:T(128)S(6)} %select_n.52, bf16[16,4096]{1,0:T(8,128)(2,1)S(1)} %get-tuple-element.574, f32[4096]{0:T(1024)S(1)} %bitcast.54, f32[512]{0:T(512)S(1)} %dynamic_slice.72, f32[4096]{0:T(1024)S(1)} %get-tuple-element.571, ...), kind=kOutput, calls=%fused_computation.4.clone.1 | convolution fusion | flops 88080384 | bytes 233476 | tf_op jit(solution)/shard_map/while/body/eval_jaxpr/dot_general | solution.py:43
  6.5 3.0 %fusion.37 = f32[16,4096]{1,0:T(8,128)S(1)} fusion(f32[16,4096]{1,0:T(8,128)S(1)} %get-tuple-element.554, s32[]{:T(128)S(6)} %select_n.52, bf16[16,4096]{1,0:T(8,128)(2,1)S(1)} %get-tuple-element.574, f32[4096]{0:T(1024)S(1)} %bitcast.54, f32[512]{0:T(512)S(1)} %dynamic_slice.72, f32[4096]{0:T(1024)S(1)} %get-tuple-element.571, ...), kind=kOutput, calls=%fused_computation.4.clone.1 | convolution fusion | flops 88080384 | bytes 233476 | tf_op jit(solution)/shard_map/while/body/eval_jaxpr/dot_general | solution.py:43
  9.7 3.0 %fusion.37 = f32[16,4096]{1,0:T(8,128)S(1)} fusion(f32[16,4096]{1,0:T(8,128)S(1)} %get-tuple-element.554, s32[]{:T(128)S(6)} %select_n.52, bf16[16,4096]{1,0:T(8,128)(2,1)S(1)} %get-tuple-element.574, f32[4096]{0:T(1024)S(1)} %bitcast.54, f32[512]{0:T(512)S(1)} %dynamic_slice.72, f32[4096]{0:T(1024)S(1)} %get-tuple-element.571, ...), kind=kOutput, calls=%fused_computation.4.clone.1 | convolution fusion | flops 88080384 | bytes 233476 | tf_op jit(solution)/shard_map/while/body/eval_jaxpr/dot_general | solution.py:43
  12.9 3.0 %fusion.37 = f32[16,4096]{1,0:T(8,128)S(1)} fusion(f32[16,4096]{1,0:T(8,128)S(1)} %get-tuple-element.554, s32[]{:T(128)S(6)} %select_n.52, bf16[16,4096]{1,0:T(8,128)(2,1)S(1)} %get-tuple-element.574, f32[4096]{0:T(1024)S(1)} %bitcast.54, f32[512]{0:T(512)S(1)} %dynamic_slice.72, f32[4096]{0:T(1024)S(1)} %get-tuple-element.571, ...), kind=kOutput, calls=%fused_computation.4.clone.1 | convolution fusion | flops 88080384 | bytes 233476 | tf_op jit(solution)/shard_map/while/body/eval_jaxpr/dot_general | solution.py:43
  16.1 3.0 %fusion.37 = f32[16,4096]{1,0:T(8,128)S(1)} fusion(f32[16,4096]{1,0:T(8,128)S(1)} %get-tuple-element.554, s32[]{:T(128)S(6)} %select_n.52, bf16[16,4096]{1,0:T(8,128)(2,1)S(1)} %get-tuple-element.574, f32[4096]{0:T(1024)S(1)} %bitcast.54, f32[512]{0:T(512)S(1)} %dynamic_slice.72, f32[4096]{0:T(1024)S(1)} %get-tuple-element.571, ...), kind=kOutput, calls=%fused_computation.4.clone.1 | convolution fusion | flops 88080384 | bytes 233476 | tf_op jit(solution)/shard_map/while/body/eval_jaxpr/dot_general | solution.py:43
  19.3 3.0 %fusion.37 = f32[16,4096]{1,0:T(8,128)S(1)} fusion(f32[16,4096]{1,0:T(8,128)S(1)} %get-tuple-element.554, s32[]{:T(128)S(6)} %select_n.52, bf16[16,4096]{1,0:T(8,128)(2,1)S(1)} %get-tuple-element.574, f32[4096]{0:T(1024)S(1)} %bitcast.54, f32[512]{0:T(512)S(1)} %dynamic_slice.72, f32[4096]{0:T(1024)S(1)} %get-tuple-element.571, ...), kind=kOutput, calls=%fused_computation.4.clone.1 | convolution fusion | flops 88080384 | bytes 233476 | tf_op jit(solution)/shard_map/while/body/eval_jaxpr/dot_general | solution.py:43
  22.4 3.0 %fusion.37 = f32[16,4096]{1,0:T(8,128)S(1)} fusion(f32[16,4096]{1,0:T(8,128)S(1)} %get-tuple-element.554, s32[]{:T(128)S(6)} %select_n.52, bf16[16,4096]{1,0:T(8,128)(2,1)S(1)} %get-tuple-element.574, f32[4096]{0:T(1024)S(1)} %bitcast.54, f32[512]{0:T(512)S(1)} %dynamic_slice.72, f32[4096]{0:T(1024)S(1)} %get-tuple-element.571, ...), kind=kOutput, calls=%fused_computation.4.clone.1 | convolution fusion | flops 88080384 | bytes 233476 | tf_op jit(solution)/shard_map/while/body/eval_jaxpr/dot_general | solution.py:43
  25.6 3.0 %fusion.37 = f32[16,4096]{1,0:T(8,128)S(1)} fusion(f32[16,4096]{1,0:T(8,128)S(1)} %get-tuple-element.554, s32[]{:T(128)S(6)} %select_n.52, bf16[16,4096]{1,0:T(8,128)(2,1)S(1)} %get-tuple-element.574, f32[4096]{0:T(1024)S(1)} %bitcast.54, f32[512]{0:T(512)S(1)} %dynamic_slice.72, f32[4096]{0:T(1024)S(1)} %get-tuple-element.571, ...), kind=kOutput, calls=%fused_computation.4.clone.1 | convolution fusion | flops 88080384 | bytes 233476 | tf_op jit(solution)/shard_map/while/body/eval_jaxpr/dot_general | solution.py:43
  28.7 0.2 copy.31
  28.9 0.9 copy.32
  29.8 16.6 %all-to-all-start = ((f32[128,4,128]{2,1,0:T(4,128)}), f32[128,4,128]{2,1,0:T(4,128)S(1)}, u32[]{:S(2)}, u32[]{:S(2)}) async-start(f32[128,4,128]{2,1,0:T(4,128)} %copy.32), calls=%async_computation | async-start | bytes 524288 | tf_op jit(solution)/shard_map/all_to_all | solution.py:79
  46.5 0.8 dynamic-slice_multiply_fusion
  47.3 12.0 %all-to-all-done = f32[128,4,128]{2,1,0:T(4,128)S(1)} async-done(((f32[128,4,128]{2,1,0:T(4,128)}), f32[128,4,128]{2,1,0:T(4,128)S(1)}, u32[]{:S(2)}, u32[]{:S(2)}) %all-to-all-start) | async-done | bytes 262176 | tf_op jit(solution)/shard_map/all_to_all | solution.py:79
  59.2 0.1 reduce_sum.36
  59.4 0.7 broadcast_in_dim.57
  60.0 6.6 %all-to-all-start.1 = ((bf16[128,4,128]{2,1,0:T(4,128)(2,1)}), bf16[128,4,128]{2,1,0:T(4,128)(2,1)S(1)}, u32[]{:S(2)}, u32[]{:S(2)}) async-start(bf16[128,4,128]{2,1,0:T(4,128)(2,1)} %broadcast_in_dim.57), calls=%async_computation.1 | async-start | bytes 262144 | tf_op jit(solution)/shard_map/all_to_all | solution.py:79
  66.7 10.9 %all-to-all-done.1 = bf16[128,4,128]{2,1,0:T(4,128)(2,1)S(1)} async-done(((bf16[128,4,128]{2,1,0:T(4,128)(2,1)}), bf16[128,4,128]{2,1,0:T(4,128)(2,1)S(1)}, u32[]{:S(2)}, u32[]{:S(2)}) %all-to-all-start.1) | async-done | bytes 131104 | tf_op jit(solution)/shard_map/all_to_all | solution.py:79
  77.7 25.6 %while.30 = (s32[]{:T(128)}, f32[16,4096]{1,0:T(8,128)S(1)}, bf16[16,4096]{1,0:T(8,128)(2,1)S(1)}, f32[4096]{0:T(1024)S(1)}, f32[4096]{0:T(1024)S(1)}, /*index=5...) while((s32[]{:T(128)}, f32[16,4096]{1,0:T(8,128)S(1)}, ...), condition=%wide.region_4.5_spmd.clone, body=%wide.region_3.4_spmd.clone.sunk | while | flops 88215560 | bytes 651457 | solution.py:66
  77.7 0.1 dynamic_slice.75
  77.9 3.0 %convolution_add_fusion.2 = f32[16,4096]{1,0:T(8,128)S(1)} fusion(f32[4096]{0:T(1024)S(1)} %bitcast.55, f32[512]{0:T(512)S(1)} %dynamic_slice.75, f32[4096]{0:T(1024)S(1)} %get-tuple-element.611, f32[512]{0:T(512)S(1)} %dynamic_slice.76, f32[4096]{0:T(1024)S(1)} %get-tuple-element.609, f32[4096]{0:T(1024)S(1)} %broadcast_multiply_fusion.6, ...), kind=kOutput, calls=%fused_computation.8.clone.1 | convolution fusion | flops 88211456 | bytes 610309 | tf_op jit(solution)/shard_map/while/body/eval_jaxpr/dot_general | solution.py:64
  80.9 0.1 dynamic_slice.75
  81.1 3.0 %convolution_add_fusion.2 = f32[16,4096]{1,0:T(8,128)S(1)} fusion(f32[4096]{0:T(1024)S(1)} %bitcast.55, f32[512]{0:T(512)S(1)} %dynamic_slice.75, f32[4096]{0:T(1024)S(1)} %get-tuple-element.611, f32[512]{0:T(512)S(1)} %dynamic_slice.76, f32[4096]{0:T(1024)S(1)} %get-tuple-element.609, f32[4096]{0:T(1024)S(1)} %broadcast_multiply_fusion.6, ...), kind=kOutput, calls=%fused_computation.8.clone.1 | convolution fusion | flops 88211456 | bytes 610309 | tf_op jit(solution)/shard_map/while/body/eval_jaxpr/dot_general | solution.py:64
  84.3 3.0 %convolution_add_fusion.2 = f32[16,4096]{1,0:T(8,128)S(1)} fusion(f32[4096]{0:T(1024)S(1)} %bitcast.55, f32[512]{0:T(512)S(1)} %dynamic_slice.75, f32[4096]{0:T(1024)S(1)} %get-tuple-element.611, f32[512]{0:T(512)S(1)} %dynamic_slice.76, f32[4096]{0:T(1024)S(1)} %get-tuple-element.609, f32[4096]{0:T(1024)S(1)} %broadcast_multiply_fusion.6, ...), kind=kOutput, calls=%fused_computation.8.clone.1 | convolution fusion | flops 88211456 | bytes 610309 | tf_op jit(solution)/shard_map/while/body/eval_jaxpr/dot_general | solution.py:64
  87.5 3.0 %convolution_add_fusion.2 = f32[16,4096]{1,0:T(8,128)S(1)} fusion(f32[4096]{0:T(1024)S(1)} %bitcast.55, f32[512]{0:T(512)S(1)} %dynamic_slice.75, f32[4096]{0:T(1024)S(1)} %get-tuple-element.611, f32[512]{0:T(512)S(1)} %dynamic_slice.76, f32[4096]{0:T(1024)S(1)} %get-tuple-element.609, f32[4096]{0:T(1024)S(1)} %broadcast_multiply_fusion.6, ...), kind=kOutput, calls=%fused_computation.8.clone.1 | convolution fusion | flops 88211456 | bytes 610309 | tf_op jit(solution)/shard_map/while/body/eval_jaxpr/dot_general | solution.py:64
  90.7 3.0 %convolution_add_fusion.2 = f32[16,4096]{1,0:T(8,128)S(1)} fusion(f32[4096]{0:T(1024)S(1)} %bitcast.55, f32[512]{0:T(512)S(1)} %dynamic_slice.75, f32[4096]{0:T(1024)S(1)} %get-tuple-element.611, f32[512]{0:T(512)S(1)} %dynamic_slice.76, f32[4096]{0:T(1024)S(1)} %get-tuple-element.609, f32[4096]{0:T(1024)S(1)} %broadcast_multiply_fusion.6, ...), kind=kOutput, calls=%fused_computation.8.clone.1 | convolution fusion | flops 88211456 | bytes 610309 | tf_op jit(solution)/shard_map/while/body/eval_jaxpr/dot_general | solution.py:64
  93.9 3.0 %convolution_add_fusion.2 = f32[16,4096]{1,0:T(8,128)S(1)} fusion(f32[4096]{0:T(1024)S(1)} %bitcast.55, f32[512]{0:T(512)S(1)} %dynamic_slice.75, f32[4096]{0:T(1024)S(1)} %get-tuple-element.611, f32[512]{0:T(512)S(1)} %dynamic_slice.76, f32[4096]{0:T(1024)S(1)} %get-tuple-element.609, f32[4096]{0:T(1024)S(1)} %broadcast_multiply_fusion.6, ...), kind=kOutput, calls=%fused_computation.8.clone.1 | convolution fusion | flops 88211456 | bytes 610309 | tf_op jit(solution)/shard_map/while/body/eval_jaxpr/dot_general | solution.py:64
  97.1 3.0 %convolution_add_fusion.2 = f32[16,4096]{1,0:T(8,128)S(1)} fusion(f32[4096]{0:T(1024)S(1)} %bitcast.55, f32[512]{0:T(512)S(1)} %dynamic_slice.75, f32[4096]{0:T(1024)S(1)} %get-tuple-element.611, f32[512]{0:T(512)S(1)} %dynamic_slice.76, f32[4096]{0:T(1024)S(1)} %get-tuple-element.609, f32[4096]{0:T(1024)S(1)} %broadcast_multiply_fusion.6, ...), kind=kOutput, calls=%fused_computation.8.clone.1 | convolution fusion | flops 88211456 | bytes 610309 | tf_op jit(solution)/shard_map/while/body/eval_jaxpr/dot_general | solution.py:64
  100.3 3.0 %convolution_add_fusion.2 = f32[16,4096]{1,0:T(8,128)S(1)} fusion(f32[4096]{0:T(1024)S(1)} %bitcast.55, f32[512]{0:T(512)S(1)} %dynamic_slice.75, f32[4096]{0:T(1024)S(1)} %get-tuple-element.611, f32[512]{0:T(512)S(1)} %dynamic_slice.76, f32[4096]{0:T(1024)S(1)} %get-tuple-element.609, f32[4096]{0:T(1024)S(1)} %broadcast_multiply_fusion.6, ...), kind=kOutput, calls=%fused_computation.8.clone.1 | convolution fusion | flops 88211456 | bytes 610309 | tf_op jit(solution)/shard_map/while/body/eval_jaxpr/dot_general | solution.py:64
  103.3 0.2 reshape.105
  103.5 0.8 copy.35
  104.4 5.9 %all-to-all-start.2 = ((f32[4,16,1024]{2,1,0:T(8,128)}), f32[4,16,1024]{2,1,0:T(8,128)S(1)}, u32[]{:S(2)}, u32[]{:S(2)}) async-start(f32[4,16,1024]{2,1,0:T(8,128)} %copy.35), calls=%async_computation.2 | async-start | bytes 524288 | tf_op jit(solution)/shard_map/all_to_all | solution.py:79
  110.3 0.7 dynamic_slice.50
  111.0 7.9 %all-to-all-done.2 = f32[4,16,1024]{2,1,0:T(8,128)S(1)} async-done(((f32[4,16,1024]{2,1,0:T(8,128)}), f32[4,16,1024]{2,1,0:T(8,128)S(1)}, u32[]{:S(2)}, u32[]{:S(2)}) %all-to-all-start.2) | async-done | bytes 262176 | tf_op jit(solution)/shard_map/all_to_all | solution.py:79
  118.9 0.2 fusion.19
  119.0 0.1 broadcast_in_dim.58
  119.2 16.4 %all_to_all.25 = f32[32,2,128]{2,1,0:T(2,128)S(1)} all-to-all(f32[32,2,128]{2,1,0:T(2,128)S(1)} %broadcast_in_dim.59), channel_id=1, replica_groups=mesh['z'=8,'yl'=2,'x'=4,'c'=2,'yh'=4] {'x','c','yh'}, dimensions={0} | all-to-all | bytes 65536 | tf_op jit(solution)/shard_map/all_to_all | solution.py:79
  135.6 10.2 %all_to_all.26 = f32[16,2,128]{2,1,0:T(2,128)S(1)} all-to-all(f32[16,2,128]{2,1,0:T(2,128)S(1)} %broadcast_in_dim.60), channel_id=1, replica_groups=mesh['z'=8,'yl'=2,'x'=4,'c'=2,'yh'=4] {'z','yl'}, dimensions={0} | all-to-all | bytes 32768 | tf_op jit(solution)/shard_map/all_to_all | solution.py:79
  145.9 0.1 div.29
  146.0 1.5 cholesky.16
  147.5 0.6 compare_reduce_fusion
  148.2 1.2 select_bitcast_fusion
  149.4 1.2 custom-call.7
  150.6 0.9 fusion.18
  (64 shorter events, 2.6 us)
Async XLA Ops:
  0.6 2.5 %copy-start = (bf16[16,4096]{1,0:T(8,128)(2,1)S(1)}, bf16[16,4096]{1,0:T(8,128)(2,1)}, u32[]{:S(2)}) copy-start(bf16[16,4096]{1,0:T(8,128)(2,1)} %param.10) | copy-start | bytes 393220
  29.8 29.4 %all-to-all-start = ((f32[128,4,128]{2,1,0:T(4,128)}), f32[128,4,128]{2,1,0:T(4,128)S(1)}, u32[]{:S(2)}, u32[]{:S(2)}) async-start(f32[128,4,128]{2,1,0:T(4,128)} %copy.32), calls=%async_computation | async-start | bytes 524288 | tf_op jit(solution)/shard_map/all_to_all | solution.py:79
  60.0 17.5 %all-to-all-start.1 = ((bf16[128,4,128]{2,1,0:T(4,128)(2,1)}), bf16[128,4,128]{2,1,0:T(4,128)(2,1)S(1)}, u32[]{:S(2)}, u32[]{:S(2)}) async-start(bf16[128,4,128]{2,1,0:T(4,128)(2,1)} %broadcast_in_dim.57), calls=%async_computation.1 | async-start | bytes 262144 | tf_op jit(solution)/shard_map/all_to_all | solution.py:79
  104.4 14.5 %all-to-all-start.2 = ((f32[4,16,1024]{2,1,0:T(8,128)}), f32[4,16,1024]{2,1,0:T(8,128)S(1)}, u32[]{:S(2)}, u32[]{:S(2)}) async-start(f32[4,16,1024]{2,1,0:T(8,128)} %copy.35), calls=%async_computation.2 | async-start | bytes 524288 | tf_op jit(solution)/shard_map/all_to_all | solution.py:79

commit v2 on v1

--- a/solution.py
+++ b/solution.py
@@ -1,16 +1,24 @@
+import functools
 import math
 
 import jax
 import jax.numpy as jnp
 from jax import lax
+from jax.experimental import pallas as pl
+from jax.experimental.pallas import tpu as pltpu
 from jax.sharding import Mesh, PartitionSpec as P
 
 GRAVITY = 2.0
 JITTER = 1e-06
 SUBSTEP = 0.00390625
+K = 16
 CELL_AXES = ("z", "yl", "x", "c")
+SCATTER = ("yl", "x", "c")
+REDUCE = ("z",)
 NEAR = ("x", "c", "yh")
 FAR = ("z", "yl")
+SPAN = 1024
+VMEM = pl.BlockSpec(memory_space=pltpu.VMEM)
 
 
 def cell_points(cell_plan, cell_depth):
@@ -66,55 +74,127 @@
     return lax.fori_loop(0, station_count // block_size, transposed_advance, running)
 
 
-def gram_term(hess_image):
-    return jnp.dot(
-        hess_image,
-        hess_image.T,
+def exchanged(blocks, axes):
+    return lax.all_to_all(blocks, axes, 0, 0, tiled=True)
+
+
+def called(kernel, name, out_shape, count, limit=8 << 20):
+    outs = VMEM if not isinstance(out_shape, tuple) else (VMEM,) * len(out_shape)
+    return pl.pallas_call(
+        kernel,
+        out_shape=out_shape,
+        in_specs=[VMEM] * count,
+        out_specs=outs,
+        compiler_params=pltpu.CompilerParams(vmem_limit_bytes=limit),
+        name=name,
+    )
+
+
+def sum_of(ref):
+    total = ref[0]
+    for i in range(1, ref.shape[0]):
+        total = total + ref[i]
+    return total
+
+
+def copies_kernel(parts_ref, copies_ref):
+    total = sum_of(parts_ref)
+    for i in range(copies_ref.shape[0]):
+        copies_ref[i] = total
+
+
+def weigh_kernel(parts_ref, weight_ref, copies_ref):
+    weight = weight_ref[...]
+    total = ((weight * weight) * sum_of(parts_ref)).astype(jnp.bfloat16)
+    for i in range(copies_ref.shape[0]):
+        copies_ref[i] = total
+
+
+def gram_kernel(parts_ref, reg_ref, probes_ref, image_ref, copies_ref):
+    image = sum_of(parts_ref) + reg_ref[...] * probes_ref[...].astype(jnp.float32)
+    image_ref[...] = image
+    wide = lax.dot_general(
+        image,
+        jnp.concatenate([image] * 8, axis=0),
+        (((1,), (1,)), ((), ())),
         precision=lax.Precision.HIGHEST,
         preferred_element_type=jnp.float32,
     )
-
-
-def exchanged(blocks, axes):
-    return lax.all_to_all(blocks, axes, 0, 0, tiled=True)
-
-
-def group_sum(value, axes):
-    copies = jnp.broadcast_to(value[None], (lax.axis_size(axes), *value.shape))
-    return jnp.sum(exchanged(copies, axes), axis=0)
+    sub = lax.broadcasted_iota(jnp.int32, (K, 128), 0)
+    lane = lax.broadcasted_iota(jnp.int32, (K, 128), 1)
+    kept = jnp.where(lane // K == sub % 8, wide, 0.0)
+    for half in range(2):
+        packed = jnp.sum(kept[half * 8 : (half + 1) * 8, :], axis=0, keepdims=True)
+        for i in range(copies_ref.shape[0]):
+            copies_ref[i, half : half + 1, :] = packed
+
+
+def solve_kernel(cell_total, parts_ref, image_ref, basis_ref, factor_ref):
+    packed = sum_of(parts_ref)
+    sub = lax.broadcasted_iota(jnp.int32, (K, 128), 0)
+    lane = lax.broadcasted_iota(jnp.int32, (K, 128), 1)
+    rows = jnp.concatenate([jnp.broadcast_to(packed[h : h + 1, :], (8, 128)) for h in range(2)], axis=0)
+    rows = jnp.where(lane // K == sub % 8, rows, 0.0)
+    for shift in (16, 32, 64):
+        rows = rows + pltpu.roll(rows, shift, 1)
+    matrix = rows / cell_total + jnp.where(lane == sub, JITTER, 0.0)
+    right = image_ref[...]
+    lower = jnp.zeros((K, 128), jnp.float32)
+    for j in range(K):
+        pivot = jnp.broadcast_to(matrix[j : j + 1, j : j + 1], (1, 128))
+        scale = lax.rsqrt(pivot)
+        scale = scale * (1.5 - 0.5 * pivot * scale * scale)
+        column = jnp.where(sub >= j, jnp.broadcast_to(matrix[:, j : j + 1], (K, 128)) * scale, 0.0)
+        lower = jnp.where(lane == j, column, lower)
+        row = matrix[j : j + 1, :] * scale
+        right_row = right[j : j + 1, :] * scale[:, 0:1]
+        basis_ref[j : j + 1, :] = right_row
+        if j + 1 < K:
+            matrix = matrix - column * row
+            right = right - column[:, 0:1] * right_row
+    factor_ref[...] = lower[:, 0:K]
 
 
 def body(probes, reg_weight, cell_plan, cell_depth, station_index, station_weight):
+    f32 = jnp.float32
     cell_geom = cell_points(cell_plan, cell_depth)
-    st_east = station_index[0].astype(jnp.float32) * SUBSTEP
-    st_north = station_index[1].astype(jnp.float32) * SUBSTEP
-    station_scale = station_weight * station_weight
+    st_east = station_index[0].astype(f32) * SUBSTEP
+    st_north = station_index[1].astype(f32) * SUBSTEP
+    cells, stations = probes.shape[1], station_index.shape[1]
     terms = forward_terms(probes, st_east, st_north, cell_geom)
-    blocks = terms.reshape(2, 2, 4, 32, 128).transpose(0, 3, 1, 2, 4).reshape(128, 4, 128)
-    own_field = jnp.sum(exchanged(blocks, CELL_AXES), axis=0)
-    own_block = (lax.axis_index(CELL_AXES) % 64) // 2
-    own_scale = lax.dynamic_slice_in_dim(station_scale, own_block * 128, 128)
-    own_weighted = (own_scale[None, :] * own_field).astype(jnp.bfloat16)
-    gathered = exchanged(jnp.broadcast_to(own_weighted[None], (128, 4, 128)), CELL_AXES)
-    weighted = gathered.reshape(2, 32, 2, 4, 128).transpose(0, 2, 3, 1, 4).reshape(16, 4096)
-    zero_image = jnp.zeros((probes.shape[0], probes.shape[1]), jnp.float32)
-    backward = transposed_add(zero_image, weighted, st_east, st_north, cell_geom)
-    group_count = lax.axis_size("yh")
-    quarter = probes.shape[1] // group_count
-    offset_cells = lax.axis_index("yh") * quarter
-    cell_total = probes.shape[1] * lax.axis_size(CELL_AXES)
-    parts = backward.reshape(16, group_count, quarter).transpose(1, 0, 2)
-    summed = jnp.sum(exchanged(parts, "yh"), axis=0)
-    own_reg = lax.dynamic_slice_in_dim(reg_weight, offset_cells, quarter)
-    own_probes = lax.dynamic_slice_in_dim(probes, offset_cells, quarter, 1)
-    local_image = summed + own_reg[None, :] * own_probes.astype(jnp.float32)
-    gram_flat = gram_term(local_image).reshape(2, 128)
-    gram_flat = group_sum(group_sum(gram_flat, NEAR), FAR)
-    gram_matrix = gram_flat.reshape(16, 16)
-    gram_matrix = gram_matrix / cell_total + JITTER * jnp.eye(probes.shape[0], dtype=jnp.float32)
-    lower_factor = jnp.linalg.cholesky(gram_matrix)
-    basis_rows = jax.scipy.linalg.solve_triangular(lower_factor, local_image, lower=True)
-    return (basis_rows, lower_factor)
+    blocks = lax.axis_size(SCATTER)
+    across = blocks // 2
+    width = stations // across
+    field = terms.reshape(2, 8, across, width).transpose(0, 2, 1, 3).reshape(blocks, 8, width)
+    parts = exchanged(field, SCATTER)
+    count = lax.axis_size(REDUCE)
+    parts = called(copies_kernel, "reduced", jax.ShapeDtypeStruct((count, 8, width), f32), 1)(parts)
+    parts = exchanged(parts, REDUCE)
+    start = (lax.axis_index(SCATTER) % across) * width
+    own_weight = lax.dynamic_slice_in_dim(station_weight, start, width).reshape(1, width)
+    own = called(weigh_kernel, "weighed", jax.ShapeDtypeStruct((blocks, 8, width), jnp.bfloat16), 2)(parts, own_weight)
+    gathered = exchanged(own, SCATTER)
+    weighted = gathered.reshape(2, across, 8, width).transpose(0, 2, 1, 3).reshape(K, stations)
+    backward = transposed_add(jnp.zeros((K, cells), f32), weighted, st_east, st_north, cell_geom)
+    parts = exchanged(backward.reshape(K, cells // SPAN, SPAN).transpose(1, 0, 2), "yh")
+    offset = lax.axis_index("yh") * SPAN
+    own_reg = lax.dynamic_slice_in_dim(reg_weight, offset, SPAN).reshape(1, SPAN)
+    own_probes = lax.dynamic_slice_in_dim(probes, offset, SPAN, 1)
+    near, far = lax.axis_size(NEAR), lax.axis_size(FAR)
+    image, grams = called(
+        gram_kernel,
+        "gram",
+        (jax.ShapeDtypeStruct((K, SPAN), f32), jax.ShapeDtypeStruct((near, 2, 128), f32)),
+        3,
+    )(parts, own_reg, own_probes)
+    grams = called(copies_kernel, "summed", jax.ShapeDtypeStruct((far, 2, 128), f32), 1)(exchanged(grams, NEAR))
+    cell_total = float(cells * lax.axis_size(CELL_AXES))
+    return called(
+        functools.partial(solve_kernel, cell_total),
+        "solve",
+        (jax.ShapeDtypeStruct((K, SPAN), f32), jax.ShapeDtypeStruct((K, K), f32)),
+        2,
+    )(exchanged(grams, FAR), image)
 
 
 def solution(mesh):

time: 152 us -> 144 us (0.947)
  blocking collectives: 26.6 us -> 43.2 us
  starting transfers between devices: 29.2 us -> 18.8 us
  waiting for transfers between devices: 30.7 us -> 20.9 us
  other arithmetic: 8.16 us -> 2.52 us
  Pallas kernels: 0 us -> 4.19 us
  local copies, waits for them, and re-layouts: 6.32 us -> 4.58 us
    all_to_all x2 -> x3, blocking collectives: 26.6 us -> 43.2 us  [exchanged(): return lax.all_to_all(blocks, axes, 0, 0, tiled=True)]
    all_to_all x3, starting transfers between devices: 29.2 us -> 18.8 us  [exchanged(): return lax.all_to_all(blocks, axes, 0, 0, tiled=True)]
    all_to_all x3, waiting for transfers between devices: 30.7 us -> 20.9 us  [exchanged(): return lax.all_to_all(blocks, axes, 0, 0, tiled=True)]
    another operation x5 -> x0, other arithmetic: 4.61 us -> none  [the longest x2 2.47 us: body(): jax.scipy.linalg.solve_triangular(lower_factor, local_image, lower=True)]
    pallas_call x0 -> x5, Pallas kernels: none -> 4.19 us  [the longest x1 2.26 us: body(): called(functools.partial(solve_kernel, cell_total), 'solve', (jax.ShapeDt...]
where the time goes in v2:
time: 144 us
  matrix products  48.8 us (34%)
  blocking collectives  43.2 us (30%)
  waiting for transfers between devices  20.9 us (15%)
  starting transfers between devices  18.8 us (13%)
  local copies, waits for them, and re-layouts  4.58 us (3%)
  Pallas kernels  4.19 us (3%)
  other arithmetic  2.52 us (2%)
    all_to_all x3, blocking collectives, exchanged(): return lax.all_to_all(blocks, axes, 0, 0, tiled=True)  43.2 us
    dot_general x8, matrix products, transposed_advance(): jnp.dot(segment, sens_tile, preferred_element_type=jnp.float32)  24.5 us
    dot_general x8, matrix products, forward_advance(): lax.dot_general(probes, sens_tile, (((1,), (1,)), ((), ())), preferred_el...  24.4 us
    all_to_all x3, waiting for transfers between devices, exchanged(): return lax.all_to_all(blocks, axes, 0, 0, tiled=True)  20.9 us
    all_to_all x3, starting transfers between devices, exchanged(): return lax.all_to_all(blocks, axes, 0, 0, tiled=True)  18.8 us
  transfers between devices with their start and end apart: 3, of which 3 were waited for; matrix products, arithmetic and copies ran while one was open for 1% of the time, Pallas kernels for 0%

profile of v2, /device:TPU:1, one launch (start us, length us, event | category | flops | bytes accessed | tf_op | source)
XLA Modules:
  0.0 143.8 jit_solution(13793674030887772582)
XLA Ops:
  0.6 0.9 convert_add_fusion
  1.5 0.9 convert_multiply_fusion
  2.4 0.7 fusion.18
  3.1 25.6 %while.29 = (s32[]{:T(128)}, f32[16,4096]{1,0:T(8,128)S(1)}, f32[4096]{0:T(1024)S(1)}, f32[4096]{0:T(1024)S(1)}, f32[4096]{0:T(1024)S(1)}, /*index=5*/f32[4096]{...) while((s32[]{:T(128)}, f32[16,4096]{1,0:T(8,128)S(1)}, ...), condition=%wide.region_1.0_spmd, body=%wide.region_0.0_spmd.sunk | while | flops 88084488 | bytes 274615 | solution.py:57
  3.2 0.1 dynamic_slice.63
  3.2 0.1 dynamic_slice.64
  3.3 3.0 %fusion.27 = f32[16,4096]{1,0:T(8,128)S(1)} fusion(f32[16,4096]{1,0:T(8,128)S(1)} %get-tuple-element.556, s32[]{:T(128)S(6)} %select_n.40, bf16[16,4096]{1,0:T(8,128)(2,1)S(1)} %get-tuple-element.576, f32[4096]{0:T(1024)S(1)} %bitcast.47, f32[512]{0:T(512)S(1)} %dynamic_slice.63, f32[4096]{0:T(1024)S(1)} %get-tuple-element.573, ...), kind=kOutput, calls=%fused_computation.4.clone.1 | convolution fusion | flops 88080384 | bytes 233476 | tf_op jit(solution)/shard_map/while/body/eval_jaxpr/dot_general | solution.py:51
  6.4 0.1 dynamic_slice.63
  6.4 0.1 dynamic_slice.64
  6.5 3.0 %fusion.27 = f32[16,4096]{1,0:T(8,128)S(1)} fusion(f32[16,4096]{1,0:T(8,128)S(1)} %get-tuple-element.556, s32[]{:T(128)S(6)} %select_n.40, bf16[16,4096]{1,0:T(8,128)(2,1)S(1)} %get-tuple-element.576, f32[4096]{0:T(1024)S(1)} %bitcast.47, f32[512]{0:T(512)S(1)} %dynamic_slice.63, f32[4096]{0:T(1024)S(1)} %get-tuple-element.573, ...), kind=kOutput, calls=%fused_computation.4.clone.1 | convolution fusion | flops 88080384 | bytes 233476 | tf_op jit(solution)/shard_map/while/body/eval_jaxpr/dot_general | solution.py:51
  9.7 3.0 %fusion.27 = f32[16,4096]{1,0:T(8,128)S(1)} fusion(f32[16,4096]{1,0:T(8,128)S(1)} %get-tuple-element.556, s32[]{:T(128)S(6)} %select_n.40, bf16[16,4096]{1,0:T(8,128)(2,1)S(1)} %get-tuple-element.576, f32[4096]{0:T(1024)S(1)} %bitcast.47, f32[512]{0:T(512)S(1)} %dynamic_slice.63, f32[4096]{0:T(1024)S(1)} %get-tuple-element.573, ...), kind=kOutput, calls=%fused_computation.4.clone.1 | convolution fusion | flops 88080384 | bytes 233476 | tf_op jit(solution)/shard_map/while/body/eval_jaxpr/dot_general | solution.py:51
  12.9 3.0 %fusion.27 = f32[16,4096]{1,0:T(8,128)S(1)} fusion(f32[16,4096]{1,0:T(8,128)S(1)} %get-tuple-element.556, s32[]{:T(128)S(6)} %select_n.40, bf16[16,4096]{1,0:T(8,128)(2,1)S(1)} %get-tuple-element.576, f32[4096]{0:T(1024)S(1)} %bitcast.47, f32[512]{0:T(512)S(1)} %dynamic_slice.63, f32[4096]{0:T(1024)S(1)} %get-tuple-element.573, ...), kind=kOutput, calls=%fused_computation.4.clone.1 | convolution fusion | flops 88080384 | bytes 233476 | tf_op jit(solution)/shard_map/while/body/eval_jaxpr/dot_general | solution.py:51
  16.1 3.0 %fusion.27 = f32[16,4096]{1,0:T(8,128)S(1)} fusion(f32[16,4096]{1,0:T(8,128)S(1)} %get-tuple-element.556, s32[]{:T(128)S(6)} %select_n.40, bf16[16,4096]{1,0:T(8,128)(2,1)S(1)} %get-tuple-element.576, f32[4096]{0:T(1024)S(1)} %bitcast.47, f32[512]{0:T(512)S(1)} %dynamic_slice.63, f32[4096]{0:T(1024)S(1)} %get-tuple-element.573, ...), kind=kOutput, calls=%fused_computation.4.clone.1 | convolution fusion | flops 88080384 | bytes 233476 | tf_op jit(solution)/shard_map/while/body/eval_jaxpr/dot_general | solution.py:51
  19.3 3.0 %fusion.27 = f32[16,4096]{1,0:T(8,128)S(1)} fusion(f32[16,4096]{1,0:T(8,128)S(1)} %get-tuple-element.556, s32[]{:T(128)S(6)} %select_n.40, bf16[16,4096]{1,0:T(8,128)(2,1)S(1)} %get-tuple-element.576, f32[4096]{0:T(1024)S(1)} %bitcast.47, f32[512]{0:T(512)S(1)} %dynamic_slice.63, f32[4096]{0:T(1024)S(1)} %get-tuple-element.573, ...), kind=kOutput, calls=%fused_computation.4.clone.1 | convolution fusion | flops 88080384 | bytes 233476 | tf_op jit(solution)/shard_map/while/body/eval_jaxpr/dot_general | solution.py:51
  22.5 3.0 %fusion.27 = f32[16,4096]{1,0:T(8,128)S(1)} fusion(f32[16,4096]{1,0:T(8,128)S(1)} %get-tuple-element.556, s32[]{:T(128)S(6)} %select_n.40, bf16[16,4096]{1,0:T(8,128)(2,1)S(1)} %get-tuple-element.576, f32[4096]{0:T(1024)S(1)} %bitcast.47, f32[512]{0:T(512)S(1)} %dynamic_slice.63, f32[4096]{0:T(1024)S(1)} %get-tuple-element.573, ...), kind=kOutput, calls=%fused_computation.4.clone.1 | convolution fusion | flops 88080384 | bytes 233476 | tf_op jit(solution)/shard_map/while/body/eval_jaxpr/dot_general | solution.py:51
  25.7 3.0 %fusion.27 = f32[16,4096]{1,0:T(8,128)S(1)} fusion(f32[16,4096]{1,0:T(8,128)S(1)} %get-tuple-element.556, s32[]{:T(128)S(6)} %select_n.40, bf16[16,4096]{1,0:T(8,128)(2,1)S(1)} %get-tuple-element.576, f32[4096]{0:T(1024)S(1)} %bitcast.47, f32[512]{0:T(512)S(1)} %dynamic_slice.63, f32[4096]{0:T(1024)S(1)} %get-tuple-element.573, ...), kind=kOutput, calls=%fused_computation.4.clone.1 | convolution fusion | flops 88080384 | bytes 233476 | tf_op jit(solution)/shard_map/while/body/eval_jaxpr/dot_general | solution.py:51
  28.8 16.5 %all_to_all.30.parts_ref = f32[16,8,512]{2,1,0:T(8,128)S(1)} all-to-all(f32[16,8,512]{2,1,0:T(8,128)S(1)} %bitcast.41), channel_id=1, replica_groups=mesh['z'=8,'yl'=2,'x'=4,'c'=2,'yh'=4] {'yl','x','c'}, dimensions={0} | all-to-all | bytes 524288 | tf_op jit(solution)/shard_map/all_to_all | solution.py:78
  45.3 0.7 reduced.1
  46.0 7.3 %all-to-all-start.1 = ((f32[8,8,512]{2,1,0:T(8,128)}), f32[8,8,512]{2,1,0:T(8,128)S(1)}, u32[]{:S(2)}, u32[]{:S(2)}) async-start(f32[8,8,512]{2,1,0:T(8,128)} %reduced.1), calls=%async_computation.1 | async-start | bytes 262144 | tf_op jit(solution)/shard_map/all_to_all | solution.py:78
  53.3 0.8 dynamic_slice.49
  54.0 7.3 %all-to-all-done.1.parts_ref = f32[8,8,512]{2,1,0:T(8,128)S(1)} async-done(((f32[8,8,512]{2,1,0:T(8,128)}), f32[8,8,512]{2,1,0:T(8,128)S(1)}, u32[]{:S(2)}, u32[]{:S(2)}) %all-to-all-start.1) | async-done | bytes 131104 | tf_op jit(solution)/shard_map/all_to_all | solution.py:78
  61.3 0.7 weighed.1
  62.0 5.6 %all-to-all-start.2 = ((bf16[16,8,512]{2,1,0:T(8,128)(2,1)}), bf16[16,8,512]{2,1,0:T(8,128)(2,1)S(1)}, u32[]{:S(2)}, u32[]{:S(2)}) async-start(bf16[16,8,512]{2,1,0:T(8,128)(2,1)} %weighed.1), calls=%async_computation.2 | async-start | bytes 262144 | tf_op jit(solution)/shard_map/all_to_all | solution.py:78
  67.6 6.2 %all-to-all-done.2 = bf16[16,8,512]{2,1,0:T(8,128)(2,1)S(1)} async-done(((bf16[16,8,512]{2,1,0:T(8,128)(2,1)}), bf16[16,8,512]{2,1,0:T(8,128)(2,1)S(1)}, u32[]{:S(2)}, u32[]{:S(2)}) %all-to-all-start.2) | async-done | bytes 131104 | tf_op jit(solution)/shard_map/all_to_all | solution.py:78
  73.8 25.7 %while.30 = (s32[]{:T(128)}, f32[16,4096]{1,0:T(8,128)S(1)}, bf16[16,4096]{1,0:T(8,128)(2,1)S(1)}, f32[4096]{0:T(1024)S(1)}, f32[4096]{0:T(1024)S(1)}, /*index=5...) while((s32[]{:T(128)}, f32[16,4096]{1,0:T(8,128)S(1)}, ...), condition=%wide.region_3.4_spmd.clone, body=%wide.region_2.3_spmd.clone.sunk | while | flops 88215560 | bytes 651457 | solution.py:74
  74.0 3.1 %convolution_add_fusion.2 = f32[16,4096]{1,0:T(8,128)S(1)} fusion(f32[4096]{0:T(1024)S(1)} %bitcast.48, f32[512]{0:T(512)S(1)} %dynamic_slice.66, f32[4096]{0:T(1024)S(1)} %get-tuple-element.613, f32[512]{0:T(512)S(1)} %dynamic_slice.67, f32[4096]{0:T(1024)S(1)} %get-tuple-element.611, f32[4096]{0:T(1024)S(1)} %broadcast_multiply_fusion.5, ...), kind=kOutput, calls=%fused_computation.8.clone.1 | convolution fusion | flops 88211456 | bytes 610309 | tf_op jit(solution)/shard_map/while/body/eval_jaxpr/dot_general | solution.py:72
  77.0 0.1 dynamic_slice.66
  77.2 3.1 %convolution_add_fusion.2 = f32[16,4096]{1,0:T(8,128)S(1)} fusion(f32[4096]{0:T(1024)S(1)} %bitcast.48, f32[512]{0:T(512)S(1)} %dynamic_slice.66, f32[4096]{0:T(1024)S(1)} %get-tuple-element.613, f32[512]{0:T(512)S(1)} %dynamic_slice.67, f32[4096]{0:T(1024)S(1)} %get-tuple-element.611, f32[4096]{0:T(1024)S(1)} %broadcast_multiply_fusion.5, ...), kind=kOutput, calls=%fused_computation.8.clone.1 | convolution fusion | flops 88211456 | bytes 610309 | tf_op jit(solution)/shard_map/while/body/eval_jaxpr/dot_general | solution.py:72
  80.2 0.1 dynamic_slice.66
  80.4 3.1 %convolution_add_fusion.2 = f32[16,4096]{1,0:T(8,128)S(1)} fusion(f32[4096]{0:T(1024)S(1)} %bitcast.48, f32[512]{0:T(512)S(1)} %dynamic_slice.66, f32[4096]{0:T(1024)S(1)} %get-tuple-element.613, f32[512]{0:T(512)S(1)} %dynamic_slice.67, f32[4096]{0:T(1024)S(1)} %get-tuple-element.611, f32[4096]{0:T(1024)S(1)} %broadcast_multiply_fusion.5, ...), kind=kOutput, calls=%fused_computation.8.clone.1 | convolution fusion | flops 88211456 | bytes 610309 | tf_op jit(solution)/shard_map/while/body/eval_jaxpr/dot_general | solution.py:72
  83.4 0.1 dynamic_slice.66
  83.6 3.1 %convolution_add_fusion.2 = f32[16,4096]{1,0:T(8,128)S(1)} fusion(f32[4096]{0:T(1024)S(1)} %bitcast.48, f32[512]{0:T(512)S(1)} %dynamic_slice.66, f32[4096]{0:T(1024)S(1)} %get-tuple-element.613, f32[512]{0:T(512)S(1)} %dynamic_slice.67, f32[4096]{0:T(1024)S(1)} %get-tuple-element.611, f32[4096]{0:T(1024)S(1)} %broadcast_multiply_fusion.5, ...), kind=kOutput, calls=%fused_computation.8.clone.1 | convolution fusion | flops 88211456 | bytes 610309 | tf_op jit(solution)/shard_map/while/body/eval_jaxpr/dot_general | solution.py:72
  86.7 0.1 dynamic_slice.66
  86.8 3.1 %convolution_add_fusion.2 = f32[16,4096]{1,0:T(8,128)S(1)} fusion(f32[4096]{0:T(1024)S(1)} %bitcast.48, f32[512]{0:T(512)S(1)} %dynamic_slice.66, f32[4096]{0:T(1024)S(1)} %get-tuple-element.613, f32[512]{0:T(512)S(1)} %dynamic_slice.67, f32[4096]{0:T(1024)S(1)} %get-tuple-element.611, f32[4096]{0:T(1024)S(1)} %broadcast_multiply_fusion.5, ...), kind=kOutput, calls=%fused_computation.8.clone.1 | convolution fusion | flops 88211456 | bytes 610309 | tf_op jit(solution)/shard_map/while/body/eval_jaxpr/dot_general | solution.py:72
  89.9 0.1 dynamic_slice.66
  90.0 3.1 %convolution_add_fusion.2 = f32[16,4096]{1,0:T(8,128)S(1)} fusion(f32[4096]{0:T(1024)S(1)} %bitcast.48, f32[512]{0:T(512)S(1)} %dynamic_slice.66, f32[4096]{0:T(1024)S(1)} %get-tuple-element.613, f32[512]{0:T(512)S(1)} %dynamic_slice.67, f32[4096]{0:T(1024)S(1)} %get-tuple-element.611, f32[4096]{0:T(1024)S(1)} %broadcast_multiply_fusion.5, ...), kind=kOutput, calls=%fused_computation.8.clone.1 | convolution fusion | flops 88211456 | bytes 610309 | tf_op jit(solution)/shard_map/while/body/eval_jaxpr/dot_general | solution.py:72
  93.1 0.1 dynamic_slice.66
  93.2 3.1 %convolution_add_fusion.2 = f32[16,4096]{1,0:T(8,128)S(1)} fusion(f32[4096]{0:T(1024)S(1)} %bitcast.48, f32[512]{0:T(512)S(1)} %dynamic_slice.66, f32[4096]{0:T(1024)S(1)} %get-tuple-element.613, f32[512]{0:T(512)S(1)} %dynamic_slice.67, f32[4096]{0:T(1024)S(1)} %get-tuple-element.611, f32[4096]{0:T(1024)S(1)} %broadcast_multiply_fusion.5, ...), kind=kOutput, calls=%fused_computation.8.clone.1 | convolution fusion | flops 88211456 | bytes 610309 | tf_op jit(solution)/shard_map/while/body/eval_jaxpr/dot_general | solution.py:72
  96.3 0.1 dynamic_slice.66
  96.4 3.1 %convolution_add_fusion.2 = f32[16,4096]{1,0:T(8,128)S(1)} fusion(f32[4096]{0:T(1024)S(1)} %bitcast.48, f32[512]{0:T(512)S(1)} %dynamic_slice.66, f32[4096]{0:T(1024)S(1)} %get-tuple-element.613, f32[512]{0:T(512)S(1)} %dynamic_slice.67, f32[4096]{0:T(1024)S(1)} %get-tuple-element.611, f32[4096]{0:T(1024)S(1)} %broadcast_multiply_fusion.5, ...), kind=kOutput, calls=%fused_computation.8.clone.1 | convolution fusion | flops 88211456 | bytes 610309 | tf_op jit(solution)/shard_map/while/body/eval_jaxpr/dot_general | solution.py:72
  99.5 0.7 copy.11
  100.2 5.9 %all-to-all-start.3 = ((f32[4,16,1024]{2,1,0:T(8,128)}), f32[4,16,1024]{2,1,0:T(8,128)S(1)}, u32[]{:S(2)}, u32[]{:S(2)}) async-start(f32[4,16,1024]{2,1,0:T(8,128)} %bitcast.30), calls=%async_computation.3 | async-start | bytes 524288 | tf_op jit(solution)/shard_map/all_to_all | solution.py:78
  106.1 0.7 dynamic_slice.50
  106.8 7.4 %all-to-all-done.3.parts_ref = f32[4,16,1024]{2,1,0:T(8,128)S(1)} async-done(((f32[4,16,1024]{2,1,0:T(8,128)}), f32[4,16,1024]{2,1,0:T(8,128)S(1)}, u32[]{:S(2)}, u32[]{:S(2)}) %all-to-all-start.3) | async-done | bytes 262176 | tf_op jit(solution)/shard_map/all_to_all | solution.py:78
  114.3 0.6 gram.1
  114.8 16.7 %all_to_all.31.parts_ref = f32[32,2,128]{2,1,0:T(2,128)S(1)} all-to-all(f32[32,2,128]{2,1,0:T(2,128)S(1)} %get-tuple-element.358), channel_id=1, replica_groups=mesh['z'=8,'yl'=2,'x'=4,'c'=2,'yh'=4] {'x','c','yh'}, dimensions={0} | all-to-all | bytes 65536 | tf_op jit(solution)/shard_map/all_to_all | solution.py:78
  131.6 9.9 %all_to_all.32.parts_ref = f32[16,2,128]{2,1,0:T(2,128)S(1)} all-to-all(f32[16,2,128]{2,1,0:T(2,128)S(1)} %summed.1), channel_id=1, replica_groups=mesh['z'=8,'yl'=2,'x'=4,'c'=2,'yh'=4] {'z','yl'}, dimensions={0} | all-to-all | bytes 32768 | tf_op jit(solution)/shard_map/all_to_all | solution.py:78
  141.5 2.3 %solve.1 = (f32[16,1024]{1,0:T(8,128)}, f32[16,16]{1,0:T(8,128)}) custom-call(f32[16,2,128]{2,1,0:T(2,128)S(1)} %all_to_all.32.parts_ref, f32[16,1024]{1,0:T(8,128)S(1)} %get-tuple-element.359.image_ref), custom_call_target="tpu_custom_call" | custom-call | tf_op jit(solution)/shard_map/solve/pallas_call | solution.py:192
  (43 shorter events, 1.7 us)
Async XLA Ops:
  0.6 2.5 %copy-start = (bf16[16,4096]{1,0:T(8,128)(2,1)S(1)}, bf16[16,4096]{1,0:T(8,128)(2,1)}, u32[]{:S(2)}) copy-start(bf16[16,4096]{1,0:T(8,128)(2,1)} %param.10) | copy-start | bytes 393220
  46.0 15.3 %all-to-all-start.1 = ((f32[8,8,512]{2,1,0:T(8,128)}), f32[8,8,512]{2,1,0:T(8,128)S(1)}, u32[]{:S(2)}, u32[]{:S(2)}) async-start(f32[8,8,512]{2,1,0:T(8,128)} %reduced.1), calls=%async_computation.1 | async-start | bytes 262144 | tf_op jit(solution)/shard_map/all_to_all | solution.py:78
  62.0 11.8 %all-to-all-start.2 = ((bf16[16,8,512]{2,1,0:T(8,128)(2,1)}), bf16[16,8,512]{2,1,0:T(8,128)(2,1)S(1)}, u32[]{:S(2)}, u32[]{:S(2)}) async-start(bf16[16,8,512]{2,1,0:T(8,128)(2,1)} %weighed.1), calls=%async_computation.2 | async-start | bytes 262144 | tf_op jit(solution)/shard_map/all_to_all | solution.py:78
  100.2 14.0 %all-to-all-start.3 = ((f32[4,16,1024]{2,1,0:T(8,128)}), f32[4,16,1024]{2,1,0:T(8,128)S(1)}, u32[]{:S(2)}, u32[]{:S(2)}) async-start(f32[4,16,1024]{2,1,0:T(8,128)} %bitcast.30), calls=%async_computation.3 | async-start | bytes 524288 | tf_op jit(solution)/shard_map/all_to_all | solution.py:78

commit v3 on v2

--- a/solution.py
+++ b/solution.py
@@ -1,5 +1,4 @@
 import functools
-import math
 
 import jax
 import jax.numpy as jnp
@@ -15,63 +14,18 @@
 CELL_AXES = ("z", "yl", "x", "c")
 SCATTER = ("yl", "x", "c")
 REDUCE = ("z",)
-NEAR = ("x", "c", "yh")
-FAR = ("z", "yl")
+NEAR = ("yl", "x", "c", "yh")
+FAR = ("z",)
 SPAN = 1024
 VMEM = pl.BlockSpec(memory_space=pltpu.VMEM)
 
 
-def cell_points(cell_plan, cell_depth):
-    cell_east = cell_plan[0].astype(jnp.float32) + 0.5
-    cell_north = cell_plan[1].astype(jnp.float32) + 0.5
-    cell_down = cell_depth.astype(jnp.float32) + 1.0
-    return (cell_east, cell_north, cell_down)
-
-
 def sensitivity(st_east, st_north, cell_geom):
-    cell_east, cell_north, cell_down = cell_geom
-    d_east = cell_east[None, :] - st_east[:, None]
-    d_north = cell_north[None, :] - st_north[:, None]
-    distance = d_east * d_east + d_north * d_north + cell_down[None, :] * cell_down[None, :]
-    inverse = lax.rsqrt(distance)
-    return (GRAVITY * cell_down[None, :] * inverse * inverse * inverse).astype(jnp.bfloat16)
-
-
-def forward_terms(probes, st_east, st_north, cell_geom):
-    station_count = st_east.shape[0]
-    block_size = math.gcd(station_count, 512)
-
-    def forward_advance(turn_index, running):
-        start_at = turn_index * block_size
-        sens_tile = sensitivity(
-            lax.dynamic_slice_in_dim(st_east, start_at, block_size),
-            lax.dynamic_slice_in_dim(st_north, start_at, block_size),
-            cell_geom,
-        )
-        partial_value = lax.dot_general(
-            probes, sens_tile, (((1,), (1,)), ((), ())), preferred_element_type=jnp.float32
-        )
-        return lax.dynamic_update_slice_in_dim(running, partial_value, start_at, 1)
-
-    zero_field = jnp.zeros((probes.shape[0], station_count), jnp.float32)
-    return lax.fori_loop(0, station_count // block_size, forward_advance, zero_field)
-
-
-def transposed_add(running, weighted, st_east, st_north, cell_geom):
-    station_count = weighted.shape[1]
-    block_size = math.gcd(station_count, 512)
-
-    def transposed_advance(turn_index, current):
-        start_at = turn_index * block_size
-        sens_tile = sensitivity(
-            lax.dynamic_slice_in_dim(st_east, start_at, block_size),
-            lax.dynamic_slice_in_dim(st_north, start_at, block_size),
-            cell_geom,
-        )
-        segment = lax.dynamic_slice_in_dim(weighted, start_at, block_size, 1)
-        return current + jnp.dot(segment, sens_tile, preferred_element_type=jnp.float32)
-
-    return lax.fori_loop(0, station_count // block_size, transposed_advance, running)
+    cell_east, cell_north, down_squared, down_scaled = cell_geom
+    d_east = cell_east - st_east[:, None]
+    d_north = cell_north - st_north[:, None]
+    inverse = lax.rsqrt(d_east * d_east + d_north * d_north + down_squared)
+    return (down_scaled * inverse * inverse * inverse).astype(jnp.bfloat16)
 
 
 def exchanged(blocks, axes):
@@ -88,6 +42,20 @@
         compiler_params=pltpu.CompilerParams(vmem_limit_bytes=limit),
         name=name,
     )
+
+
+def geometry_kernel(plan_ref, depth_ref, station_ref, east_ref, north_ref, squared_ref, scaled_ref, st_east_ref, st_north_ref):
+    east_ref[...] = plan_ref[0:1, :].astype(jnp.float32) + 0.5
+    north_ref[...] = plan_ref[1:2, :].astype(jnp.float32) + 0.5
+    for i in range(depth_ref.shape[0]):
+        lanes = slice(i * 128, (i + 1) * 128)
+        down = depth_ref[i : i + 1, :].astype(jnp.float32) + 1.0
+        squared_ref[0:1, lanes] = down * down
+        scaled_ref[0:1, lanes] = GRAVITY * down
+    for i in range(st_east_ref.shape[0]):
+        lanes = slice(i * 128, (i + 1) * 128)
+        st_east_ref[i : i + 1, :] = station_ref[0:1, lanes].astype(jnp.float32) * SUBSTEP
+        st_north_ref[i : i + 1, :] = station_ref[1:2, lanes].astype(jnp.float32) * SUBSTEP
 
 
 def sum_of(ref):
@@ -157,11 +125,18 @@
 
 def body(probes, reg_weight, cell_plan, cell_depth, station_index, station_weight):
     f32 = jnp.float32
-    cell_geom = cell_points(cell_plan, cell_depth)
-    st_east = station_index[0].astype(f32) * SUBSTEP
-    st_north = station_index[1].astype(f32) * SUBSTEP
     cells, stations = probes.shape[1], station_index.shape[1]
-    terms = forward_terms(probes, st_east, st_north, cell_geom)
+    row = jax.ShapeDtypeStruct((1, cells), f32)
+    tiles = jax.ShapeDtypeStruct((stations // 128, 128), f32)
+    geometry = called(geometry_kernel, "geometry", (row, row, row, row, tiles, tiles), 3)
+    *cell_geom, st_east, st_north = geometry(cell_plan, cell_depth.reshape(-1, 128), station_index)
+    st_east, st_north = st_east.reshape(stations), st_north.reshape(stations)
+    terms = lax.dot_general(
+        probes,
+        sensitivity(st_east, st_north, cell_geom),
+        (((1,), (1,)), ((), ())),
+        preferred_element_type=f32,
+    )
     blocks = lax.axis_size(SCATTER)
     across = blocks // 2
     width = stations // across
@@ -175,7 +150,8 @@
     own = called(weigh_kernel, "weighed", jax.ShapeDtypeStruct((blocks, 8, width), jnp.bfloat16), 2)(parts, own_weight)
     gathered = exchanged(own, SCATTER)
     weighted = gathered.reshape(2, across, 8, width).transpose(0, 2, 1, 3).reshape(K, stations)
-    backward = transposed_add(jnp.zeros((K, cells), f32), weighted, st_east, st_north, cell_geom)
+    st_east, st_north, *cell_geom = lax.optimization_barrier((st_east, st_north, *cell_geom))
+    backward = jnp.dot(weighted, sensitivity(st_east, st_north, cell_geom), preferred_element_type=f32)
     parts = exchanged(backward.reshape(K, cells // SPAN, SPAN).transpose(1, 0, 2), "yh")
     offset = lax.axis_index("yh") * SPAN
     own_reg = lax.dynamic_slice_in_dim(reg_weight, offset, SPAN).reshape(1, SPAN)

time: 144 us -> 140 us (0.972)
  waiting for transfers between devices: 20.9 us -> 17.6 us
    all_to_all x3, waiting for transfers between devices: 20.9 us -> 17.6 us  [exchanged(): return lax.all_to_all(blocks, axes, 0, 0, tiled=True)]
    optimization_barrier x0 -> x4, other arithmetic: none -> 2.74 us  [body(): lax.optimization_barrier((st_east, st_north, *cell_geom))]
    dynamic_slice x32 -> x0, local copies, waits for them, and re-layouts: 2.38 us -> none  [the longest x8 0.6 us: forward_advance(): lax.dynamic_slice_in_dim(st_north, start_at, block_size)]
    unnamed x2 -> x8, local copies, waits for them, and re-layouts: 0.01 us -> 2.27 us
    mul x18 -> x0, other arithmetic: 1.65 us -> none  [the longest x1 0.87 us: body(): st_north = station_index[1].astype(f32) * SUBSTEP]
    dot_general x16 -> x2, matrix products: 48.8 us -> 48.2 us  [the longest x1 25.1 us: body(): jnp.dot(weighted, sensitivity(st_east, st_north, cell_geom), preferred_el...]
  transfers between devices with their start and end apart: 3 -> 3, of which waited for: 3 -> 3; matrix products, arithmetic and copies ran while one was open for 1% -> 3% of each run, Pallas kernels for 0% -> 0%
where the time goes in v3:
time: 140 us; the launch traced here: 139 us
  matrix products  48.2 us (34%)
  blocking collectives  42.8 us (31%)
  starting transfers between devices  18.8 us (13%)
  waiting for transfers between devices  17.6 us (13%)
  Pallas kernels  4.29 us (3%)
  local copies, waits for them, and re-layouts  4.28 us (3%)
  other arithmetic  2.74 us (2%)
    all_to_all x3, blocking collectives, exchanged(): return lax.all_to_all(blocks, axes, 0, 0, tiled=True)  42.8 us
    dot_general x1, matrix products, body(): jnp.dot(weighted, sensitivity(st_east, st_north, cell_geom), preferred_el...  25.1 us
    dot_general x1, matrix products, body(): lax.dot_general(probes, sensitivity(st_east, st_north, cell_geom), (((1,)...  23.1 us
    all_to_all x3, starting transfers between devices, exchanged(): return lax.all_to_all(blocks, axes, 0, 0, tiled=True)  18.8 us
    all_to_all x3, waiting for transfers between devices, exchanged(): return lax.all_to_all(blocks, axes, 0, 0, tiled=True)  17.6 us
  transfers between devices with their start and end apart: 3, of which 3 were waited for; matrix products, arithmetic and copies ran while one was open for 3% of the time, Pallas kernels for 0%

profile of v3, /device:TPU:1, one launch (start us, length us, event | category | flops | bytes accessed | tf_op | source)
XLA Modules:
  0.0 139.4 jit_solution(18415779704358979059)
XLA Ops:
  0.6 0.0 copy-start
  0.6 0.0 copy-start.1
  0.7 0.8 copy-done.1
  1.4 0.0 copy-start.2
  1.4 0.8 copy-done.2
  2.2 0.0 copy-start.3
  2.2 0.7 copy-done.3
  2.9 0.1 geometry.1
  3.0 0.0 copy-done
  3.0 23.1 %fusion.4 = f32[4096,16]{0,1:T(8,128)S(1)} fusion(bf16[16,4096]{1,0:T(8,128)(2,1)S(1)} %copy-done, f32[4096]{0:T(1024)S(1)} %bitcast.32, f32[4096]{0:T(1024)S(1)} %bitcast.36, f32[4096]{0:T(1024)S(1)} %bitcast.31, f32[4096]{0:T(1024)S(1)} %bitcast.34, f32[4096]{0:T(1024)S(1)} %bitcast.30, f32[4096]{0:T(1024)S(1)} %bitcast.29), kind=kOutput, calls=%fused_computation.5 | convolution fusion | flops 704643072 | bytes 491520 | tf_op jit(solution)/shard_map/dot_general | solution.py:134
  26.1 16.7 %all_to_all.30.parts_ref = f32[16,8,512]{2,1,0:T(8,128)S(1)} all-to-all(f32[16,8,512]{2,1,0:T(8,128)S(1)} %bitcast.38), channel_id=1, replica_groups=mesh['z'=8,'yl'=2,'x'=4,'c'=2,'yh'=4] {'yl','x','c'}, dimensions={0} | all-to-all | bytes 524288 | tf_op jit(solution)/shard_map/all_to_all | solution.py:32
  42.8 0.7 reduced.1
  43.4 7.3 %all-to-all-start.1 = ((f32[8,8,512]{2,1,0:T(8,128)}), f32[8,8,512]{2,1,0:T(8,128)S(1)}, u32[]{:S(2)}, u32[]{:S(2)}) async-start(f32[8,8,512]{2,1,0:T(8,128)} %reduced.1), calls=%async_computation.1 | async-start | bytes 262144 | tf_op jit(solution)/shard_map/all_to_all | solution.py:32
  50.7 0.8 dynamic_slice.9
  51.5 7.3 %all-to-all-done.1.parts_ref = f32[8,8,512]{2,1,0:T(8,128)S(1)} async-done(((f32[8,8,512]{2,1,0:T(8,128)}), f32[8,8,512]{2,1,0:T(8,128)S(1)}, u32[]{:S(2)}, u32[]{:S(2)}) %all-to-all-start.1) | async-done | bytes 131104 | tf_op jit(solution)/shard_map/all_to_all | solution.py:32
  58.8 0.7 weighed.1
  59.4 5.6 %all-to-all-start.2 = ((bf16[16,8,512]{2,1,0:T(8,128)(2,1)}), bf16[16,8,512]{2,1,0:T(8,128)(2,1)S(1)}, u32[]{:S(2)}, u32[]{:S(2)}) async-start(bf16[16,8,512]{2,1,0:T(8,128)(2,1)} %weighed.1), calls=%async_computation.2 | async-start | bytes 262144 | tf_op jit(solution)/shard_map/all_to_all | solution.py:32
  65.0 0.5 broadcast.63
  65.6 0.7 reduce.12
  66.3 0.7 reduce.13
  67.0 0.7 reduce.14
  67.7 0.7 reduce.15
  68.4 2.9 %all-to-all-done.2 = bf16[16,8,512]{2,1,0:T(8,128)(2,1)S(1)} async-done(((bf16[16,8,512]{2,1,0:T(8,128)(2,1)}), bf16[16,8,512]{2,1,0:T(8,128)(2,1)S(1)}, u32[]{:S(2)}, u32[]{:S(2)}) %all-to-all-start.2) | async-done | bytes 131104 | tf_op jit(solution)/shard_map/all_to_all | solution.py:32
  71.3 25.1 %fusion.6 = f32[4,16,1024]{2,1,0:T(8,128)} fusion(bf16[16,4096,1]{1,0,2:T(8,128)(2,1)S(1)} %bitcast.39, f32[4,1024]{1,0:T(4,128)S(1)} %add.64, f32[4096]{0:T(1024)S(1)} %bitcast.37, f32[4,1024]{1,0:T(4,128)S(1)} %sub.90, f32[4096]{0:T(1024)S(1)} %bitcast.35, f32[4,1024]{1,0:T(4,128)S(1)} %sub.86, f32[4,1024]{1,0:T(4,128)S(1)} %mul.96), kind=kOutput, calls=%fused_computation.6 | convolution fusion | flops 704643072 | bytes 491520 | tf_op jit(solution)/shard_map/dot_general | solution.py:154
  96.4 5.9 %all-to-all-start.3 = ((f32[4,16,1024]{2,1,0:T(8,128)}), f32[4,16,1024]{2,1,0:T(8,128)S(1)}, u32[]{:S(2)}, u32[]{:S(2)}) async-start(f32[4,16,1024]{2,1,0:T(8,128)} %fusion.6), calls=%async_computation.3 | async-start | bytes 524288 | tf_op jit(solution)/shard_map/all_to_all | solution.py:32
  102.3 0.7 dynamic_slice.10
  103.0 7.4 %all-to-all-done.3.parts_ref = f32[4,16,1024]{2,1,0:T(8,128)S(1)} async-done(((f32[4,16,1024]{2,1,0:T(8,128)}), f32[4,16,1024]{2,1,0:T(8,128)S(1)}, u32[]{:S(2)}, u32[]{:S(2)}) %all-to-all-start.3) | async-done | bytes 262176 | tf_op jit(solution)/shard_map/all_to_all | solution.py:32
  110.5 0.6 gram.1
  111.0 17.1 %all_to_all.31.parts_ref = f32[64,2,128]{2,1,0:T(2,128)S(1)} all-to-all(f32[64,2,128]{2,1,0:T(2,128)S(1)} %get-tuple-element.28), channel_id=1, replica_groups=mesh['z'=8,'yl'=2,'x'=4,'c'=2,'yh'=4] {'yl','x','c','yh'}, dimensions={0} | all-to-all | bytes 131072 | tf_op jit(solution)/shard_map/all_to_all | solution.py:32
  128.1 0.1 summed.1
  128.2 8.9 %all_to_all.32.parts_ref = f32[8,2,128]{2,1,0:T(2,128)S(1)} all-to-all(f32[8,2,128]{2,1,0:T(2,128)S(1)} %summed.1), channel_id=1, replica_groups=mesh['z'=8,'yl'=2,'x'=4,'c'=2,'yh'=4] {'z'}, dimensions={0} | all-to-all | bytes 16384 | tf_op jit(solution)/shard_map/all_to_all | solution.py:32
  137.1 2.2 %solve.1 = (f32[16,1024]{1,0:T(8,128)}, f32[16,16]{1,0:T(8,128)}) custom-call(f32[8,2,128]{2,1,0:T(2,128)S(1)} %all_to_all.32.parts_ref, f32[16,1024]{1,0:T(8,128)S(1)} %get-tuple-element.29.image_ref), custom_call_target="tpu_custom_call" | custom-call | tf_op jit(solution)/shard_map/solve/pallas_call | solution.py:168
  (5 shorter events, 0.1 us)
Async XLA Ops:
  0.6 2.3 %copy-start = (bf16[16,4096]{1,0:T(8,128)(2,1)S(1)}, bf16[16,4096]{1,0:T(8,128)(2,1)}, u32[]{:S(2)}) copy-start(bf16[16,4096]{1,0:T(8,128)(2,1)} %param.6) | copy-start | bytes 393220
  0.6 0.8 copy-start.1
  1.4 0.8 copy-start.2
  2.2 0.7 copy-start.3
  43.4 15.3 %all-to-all-start.1 = ((f32[8,8,512]{2,1,0:T(8,128)}), f32[8,8,512]{2,1,0:T(8,128)S(1)}, u32[]{:S(2)}, u32[]{:S(2)}) async-start(f32[8,8,512]{2,1,0:T(8,128)} %reduced.1), calls=%async_computation.1 | async-start | bytes 262144 | tf_op jit(solution)/shard_map/all_to_all | solution.py:32
  59.4 11.8 %all-to-all-start.2 = ((bf16[16,8,512]{2,1,0:T(8,128)(2,1)}), bf16[16,8,512]{2,1,0:T(8,128)(2,1)S(1)}, u32[]{:S(2)}, u32[]{:S(2)}) async-start(bf16[16,8,512]{2,1,0:T(8,128)(2,1)} %weighed.1), calls=%async_computation.2 | async-start | bytes 262144 | tf_op jit(solution)/shard_map/all_to_all | solution.py:32
  96.4 14.0 %all-to-all-start.3 = ((f32[4,16,1024]{2,1,0:T(8,128)}), f32[4,16,1024]{2,1,0:T(8,128)S(1)}, u32[]{:S(2)}, u32[]{:S(2)}) async-start(f32[4,16,1024]{2,1,0:T(8,128)} %fusion.6), calls=%async_computation.3 | async-start | bytes 524288 | tf_op jit(solution)/shard_map/all_to_all | solution.py:32

commit v4 on v3

--- a/solution.py
+++ b/solution.py
@@ -14,9 +14,10 @@
 CELL_AXES = ("z", "yl", "x", "c")
 SCATTER = ("yl", "x", "c")
 REDUCE = ("z",)
-NEAR = ("yl", "x", "c", "yh")
-FAR = ("z",)
+NEAR = ("yl", "c", "yh")
+FAR = ("z", "x")
 SPAN = 1024
+FILLS = (1024, 512, 512)
 VMEM = pl.BlockSpec(memory_space=pltpu.VMEM)
 
 
@@ -128,8 +129,16 @@
     cells, stations = probes.shape[1], station_index.shape[1]
     row = jax.ShapeDtypeStruct((1, cells), f32)
     tiles = jax.ShapeDtypeStruct((stations // 128, 128), f32)
-    geometry = called(geometry_kernel, "geometry", (row, row, row, row, tiles, tiles), 3)
-    *cell_geom, st_east, st_north = geometry(cell_plan, cell_depth.reshape(-1, 128), station_index)
+    sources = (cell_plan, cell_depth.reshape(-1, 128), station_index)
+    *cell_geom, st_east, st_north = pl.pallas_call(
+        geometry_kernel,
+        grid=(1,),
+        out_shape=(row, row, row, row, tiles, tiles),
+        in_specs=[pl.BlockSpec(source.shape, lambda i: (0, 0)) for source in sources],
+        out_specs=(VMEM,) * 6,
+        compiler_params=pltpu.CompilerParams(vmem_limit_bytes=8 << 20),
+        name="geometry",
+    )(*sources)
     st_east, st_north = st_east.reshape(stations), st_north.reshape(stations)
     terms = lax.dot_general(
         probes,
@@ -137,21 +146,38 @@
         (((1,), (1,)), ((), ())),
         preferred_element_type=f32,
     )
+    ends = [sum(FILLS[: i + 1]) for i in range(len(FILLS))]
+
+    def kept(i, geometry):
+        here = slice(ends[i] - FILLS[i], ends[i])
+        st_east, st_north, *cell_geom = geometry
+        return sensitivity(st_east[here], st_north[here], cell_geom)
+
+    geometry = (st_east, st_north, *cell_geom)
     blocks = lax.axis_size(SCATTER)
     across = blocks // 2
     width = stations // across
     field = terms.reshape(2, 8, across, width).transpose(0, 2, 1, 3).reshape(blocks, 8, width)
-    parts = exchanged(field, SCATTER)
+    field, geometry = lax.optimization_barrier((field, geometry))
+    parts, first = lax.optimization_barrier((exchanged(field, SCATTER), kept(0, geometry)))
     count = lax.axis_size(REDUCE)
     parts = called(copies_kernel, "reduced", jax.ShapeDtypeStruct((count, 8, width), f32), 1)(parts)
-    parts = exchanged(parts, REDUCE)
+    parts, geometry = lax.optimization_barrier((parts, geometry))
+    parts, second = lax.optimization_barrier((exchanged(parts, REDUCE), kept(1, geometry)))
     start = (lax.axis_index(SCATTER) % across) * width
     own_weight = lax.dynamic_slice_in_dim(station_weight, start, width).reshape(1, width)
     own = called(weigh_kernel, "weighed", jax.ShapeDtypeStruct((blocks, 8, width), jnp.bfloat16), 2)(parts, own_weight)
-    gathered = exchanged(own, SCATTER)
+    own, geometry = lax.optimization_barrier((own, geometry))
+    gathered, third = lax.optimization_barrier((exchanged(own, SCATTER), kept(2, geometry)))
     weighted = gathered.reshape(2, across, 8, width).transpose(0, 2, 1, 3).reshape(K, stations)
-    st_east, st_north, *cell_geom = lax.optimization_barrier((st_east, st_north, *cell_geom))
-    backward = jnp.dot(weighted, sensitivity(st_east, st_north, cell_geom), preferred_element_type=f32)
+    backward = jnp.dot(
+        weighted[:, ends[-1] :],
+        sensitivity(geometry[0][ends[-1] :], geometry[1][ends[-1] :], geometry[2:]),
+        preferred_element_type=f32,
+    )
+    for i, sens in enumerate((first, second, third)):
+        segment = weighted[:, ends[i] - FILLS[i] : ends[i]]
+        backward = backward + jnp.dot(segment, sens, preferred_element_type=f32)
     parts = exchanged(backward.reshape(K, cells // SPAN, SPAN).transpose(1, 0, 2), "yh")
     offset = lax.axis_index("yh") * SPAN
     own_reg = lax.dynamic_slice_in_dim(reg_weight, offset, SPAN).reshape(1, SPAN)

time: 140 us -> 137 us (0.979)
  blocking collectives: 42.8 us -> 25.8 us
  other arithmetic: 2.74 us -> 16.7 us
  starting transfers between devices: 18.8 us -> 29.9 us
  matrix products: 48.2 us -> 41.3 us
  waiting for transfers between devices: 17.6 us -> 13 us
    all_to_all x3 -> x2, blocking collectives: 42.8 us -> 25.8 us  [exchanged(): return lax.all_to_all(blocks, axes, 0, 0, tiled=True)]
    convert_element_type x0 -> x3, other arithmetic: none -> 16.7 us  [sensitivity(): return (down_scaled * inverse * inverse * inverse).astype(jnp.bfloat16)]
    all_to_all x3 -> x4, starting transfers between devices: 18.8 us -> 29.9 us  [exchanged(): return lax.all_to_all(blocks, axes, 0, 0, tiled=True)]
    dot_general x1 -> x4, matrix products: 25.1 us -> 17.6 us  [the longest x1 11.5 us: body(): jnp.dot(weighted[:, ends[-1]:], sensitivity(geometry[0][ends[-1]:], geome...]
    all_to_all x3 -> x4, waiting for transfers between devices: 17.6 us -> 13 us  [exchanged(): return lax.all_to_all(blocks, axes, 0, 0, tiled=True)]
    optimization_barrier x4 -> x0, other arithmetic: 2.74 us -> none  [body(): lax.optimization_barrier((st_east, st_north, *cell_geom))]
  transfers between devices with their start and end apart: 3 -> 4, of which waited for: 3 -> 3; matrix products, arithmetic and copies ran while one was open for 3% -> 13% of each run, Pallas kernels for 0% -> 0%
where the time goes in v4:
time: 137 us
  matrix products  41.3 us (30%)
  starting transfers between devices  29.9 us (22%)
  blocking collectives  25.8 us (19%)
  other arithmetic  16.7 us (12%)
  waiting for transfers between devices  13 us (9%)
  local copies, waits for them, and re-layouts  4.92 us (4%)
  Pallas kernels  4.24 us (3%)
    all_to_all x4, starting transfers between devices, exchanged(): return lax.all_to_all(blocks, axes, 0, 0, tiled=True)  29.9 us
    all_to_all x2, blocking collectives, exchanged(): return lax.all_to_all(blocks, axes, 0, 0, tiled=True)  25.8 us
    dot_general x1, matrix products, body(): lax.dot_general(probes, sensitivity(st_east, st_north, cell_geom), (((1,)...  23.7 us
    convert_element_type x3, other arithmetic, sensitivity(): return (down_scaled * inverse * inverse * inverse).astype(jnp.bfloat16)  16.7 us
    all_to_all x4, waiting for transfers between devices, exchanged(): return lax.all_to_all(blocks, axes, 0, 0, tiled=True)  13 us
    dot_general x1, matrix products, body(): jnp.dot(weighted[:, ends[-1]:], sensitivity(geometry[0][ends[-1]:], geome...  11.5 us
    dot_general x3, matrix products, body(): backward = backward + jnp.dot(segment, sens, preferred_element_type=f32)  6.06 us
  transfers between devices with their start and end apart: 4, of which 3 were waited for; matrix products, arithmetic and copies ran while one was open for 13% of the time, Pallas kernels for 0%

profile of v4, /device:TPU:1, one launch (start us, length us, event | category | flops | bytes accessed | tf_op | source)
XLA Modules:
  0.0 136.6 jit_solution(4051022828355550989)
XLA Ops:
  0.6 0.0 copy-start
  0.6 0.0 copy-start.1
  0.7 0.8 copy-done.1
  1.4 0.0 copy-start.2
  1.4 0.8 copy-done.2
  2.2 0.0 copy-start.3
  2.2 0.7 copy-done.3
  2.9 0.1 geometry.1
  3.0 0.0 copy-done
  3.0 23.7 %fusion.2 = f32[4096,16]{0,1:T(8,128)} fusion(bf16[16,4096]{1,0:T(8,128)(2,1)S(1)} %copy-done, f32[4096]{0:T(1024)S(1)} %bitcast.54, f32[4096]{0:T(1024)S(1)} %bitcast.66, f32[4096]{0:T(1024)S(1)} %bitcast.49, f32[4096]{0:T(1024)S(1)} %bitcast.71, f32[4096]{0:T(1024)S(1)} %bitcast.44, f32[4096]{0:T(1024)S(1)} %bitcast.59), kind=kOutput, calls=%fused_computation.4 | convolution fusion | flops 704643072 | bytes 491520 | tf_op jit(solution)/shard_map/dot_general | solution.py:143
  26.7 10.4 %all-to-all-start = ((f32[16,8,512]{2,1,0:T(8,128)}), f32[16,8,512]{2,1,0:T(8,128)S(1)}, u32[]{:S(2)}, u32[]{:S(2)}) async-start(f32[16,8,512]{2,1,0:T(8,128)} %bitcast.10), calls=%async_computation | async-start | bytes 524288 | tf_op jit(solution)/shard_map/all_to_all | solution.py:33
  37.1 7.7 %fusion.4 = bf16[1024,4096]{1,0:T(8,128)(2,1)} fusion(f32[4096]{0:T(1024)S(1)} %bitcast.55, f32[1024]{0:T(1024)S(1)} %slice.37, f32[4096]{0:T(1024)S(1)} %bitcast.50, f32[1024]{0:T(1024)S(1)} %slice.36, f32[4096]{0:T(1024)S(1)} %bitcast.45, f32[4096]{0:T(1024)S(1)} %bitcast.60), kind=kLoop, calls=%fused_computation.6 | loop fusion | flops 41943040 | bytes 8462336 | tf_op jit(solution)/shard_map/convert_element_type | solution.py:29
  44.8 0.8 dynamic_slice.9
  45.6 0.0 all-to-all-done.parts_ref
  45.6 0.7 reduced.1
  46.3 6.7 %all-to-all-start.1 = ((f32[8,8,512]{2,1,0:T(8,128)}), f32[8,8,512]{2,1,0:T(8,128)S(1)}, u32[]{:S(2)}, u32[]{:S(2)}) async-start(f32[8,8,512]{2,1,0:T(8,128)} %reduced.1), calls=%async_computation.1 | async-start | bytes 262144 | tf_op jit(solution)/shard_map/all_to_all | solution.py:33
  53.0 4.5 %fusion.7 = bf16[512,4096]{1,0:T(8,128)(2,1)} fusion(f32[4096]{0:T(1024)S(1)} %bitcast.56, f32[512]{0:T(512)S(1)} %slice.39, f32[4096]{0:T(1024)S(1)} %bitcast.51, f32[512]{0:T(512)S(1)} %slice.38, f32[4096]{0:T(1024)S(1)} %bitcast.46, f32[4096]{0:T(1024)S(1)} %bitcast.61), kind=kLoop, calls=%fused_computation.10 | loop fusion | flops 20971520 | bytes 4263936 | tf_op jit(solution)/shard_map/convert_element_type | solution.py:29
  57.5 3.9 %all-to-all-done.1.parts_ref = f32[8,8,512]{2,1,0:T(8,128)S(1)} async-done(((f32[8,8,512]{2,1,0:T(8,128)}), f32[8,8,512]{2,1,0:T(8,128)S(1)}, u32[]{:S(2)}, u32[]{:S(2)}) %all-to-all-start.1) | async-done | bytes 131104 | tf_op jit(solution)/shard_map/all_to_all | solution.py:33
  61.4 0.7 weighed.1
  62.1 6.9 %all-to-all-start.2 = ((bf16[16,8,512]{2,1,0:T(8,128)(2,1)}), bf16[16,8,512]{2,1,0:T(8,128)(2,1)S(1)}, u32[]{:S(2)}, u32[]{:S(2)}) async-start(bf16[16,8,512]{2,1,0:T(8,128)(2,1)} %weighed.1), calls=%async_computation.2 | async-start | bytes 262144 | tf_op jit(solution)/shard_map/all_to_all | solution.py:33
  69.0 4.5 %fusion.8 = bf16[512,4096]{1,0:T(8,128)(2,1)} fusion(f32[4096]{0:T(1024)S(1)} %bitcast.57, f32[512]{0:T(512)S(1)} %slice.41, f32[4096]{0:T(1024)S(1)} %bitcast.52, f32[512]{0:T(512)S(1)} %slice.40, f32[4096]{0:T(1024)S(1)} %bitcast.47, f32[4096]{0:T(1024)S(1)} %bitcast.62), kind=kLoop, calls=%fused_computation.11 | loop fusion | flops 20971520 | bytes 4263936 | tf_op jit(solution)/shard_map/convert_element_type | solution.py:29
  73.5 1.7 %all-to-all-done.2 = bf16[16,8,512]{2,1,0:T(8,128)(2,1)S(1)} async-done(((bf16[16,8,512]{2,1,0:T(8,128)(2,1)}), bf16[16,8,512]{2,1,0:T(8,128)(2,1)S(1)}, u32[]{:S(2)}, u32[]{:S(2)}) %all-to-all-start.2) | async-done | bytes 131104 | tf_op jit(solution)/shard_map/all_to_all | solution.py:33
  75.1 11.5 %fusion.5 = f32[16,4096]{1,0:T(8,128)S(1)} fusion(f32[4096]{0:T(1024)S(1)} %bitcast.58, f32[2048]{0:T(1024)S(1)} %slice.44, f32[4096]{0:T(1024)S(1)} %bitcast.53, f32[2048]{0:T(1024)S(1)} %slice.43, f32[4096]{0:T(1024)S(1)} %bitcast.48, f32[4096]{0:T(1024)S(1)} %bitcast.63, bf16[16,4096]{1,0:T(8,128)(2,1)S(1)} %bitcast.78), kind=kOutput, calls=%fused_computation.7 | convolution fusion | flops 352321536 | bytes 409600 | tf_op jit(solution)/shard_map/dot_general | solution.py:173
  86.7 0.0 copy-start.4
  86.7 0.0 copy-start.5
  86.7 4.7 %convolution_add_fusion.2 = f32[16,4096]{1,0:T(8,128)S(1)} fusion(f32[16,4096]{1,0:T(8,128)S(1)} %fusion.5, bf16[1024,4096]{1,0:T(8,128)(2,1)} %fusion.4, bf16[16,4096]{1,0:T(8,128)(2,1)S(1)} %bitcast.79), kind=kOutput, calls=%fused_computation.14 | convolution fusion | flops 134283264 | bytes 8945664 | tf_op jit(solution)/shard_map/dot_general | solution.py:180
  91.4 0.0 copy-done.4
  91.4 0.7 convolution_add_fusion.1
  92.1 0.4 copy-done.5
  92.5 0.7 convolution_add_fusion
  93.2 0.7 copy.11
  93.9 5.9 %all-to-all-start.3 = ((f32[4,16,1024]{2,1,0:T(8,128)}), f32[4,16,1024]{2,1,0:T(8,128)S(1)}, u32[]{:S(2)}, u32[]{:S(2)}) async-start(f32[4,16,1024]{2,1,0:T(8,128)} %bitcast.43), calls=%async_computation.3 | async-start | bytes 524288 | tf_op jit(solution)/shard_map/all_to_all | solution.py:33
  99.8 0.7 dynamic_slice.10
  100.5 7.4 %all-to-all-done.3.parts_ref = f32[4,16,1024]{2,1,0:T(8,128)S(1)} async-done(((f32[4,16,1024]{2,1,0:T(8,128)}), f32[4,16,1024]{2,1,0:T(8,128)S(1)}, u32[]{:S(2)}, u32[]{:S(2)}) %all-to-all-start.3) | async-done | bytes 262176 | tf_op jit(solution)/shard_map/all_to_all | solution.py:33
  107.9 0.5 gram.1
  108.4 13.8 %all_to_all.30.parts_ref = f32[16,2,128]{2,1,0:T(2,128)S(1)} all-to-all(f32[16,2,128]{2,1,0:T(2,128)S(1)} %get-tuple-element.70), channel_id=1, replica_groups=mesh['z'=8,'yl'=2,'x'=4,'c'=2,'yh'=4] {'yl','c','yh'}, dimensions={0} | all-to-all | bytes 32768 | tf_op jit(solution)/shard_map/all_to_all | solution.py:33
  122.2 12.1 %all_to_all.31.parts_ref = f32[32,2,128]{2,1,0:T(2,128)S(1)} all-to-all(f32[32,2,128]{2,1,0:T(2,128)S(1)} %summed.1), channel_id=1, replica_groups=mesh['z'=8,'yl'=2,'x'=4,'c'=2,'yh'=4] {'z','x'}, dimensions={0} | all-to-all | bytes 65536 | tf_op jit(solution)/shard_map/all_to_all | solution.py:33
  134.3 2.3 %solve.1 = (f32[16,1024]{1,0:T(8,128)}, f32[16,16]{1,0:T(8,128)}) custom-call(f32[32,2,128]{2,1,0:T(2,128)S(1)} %all_to_all.31.parts_ref, f32[16,1024]{1,0:T(8,128)S(1)} %get-tuple-element.71.image_ref), custom_call_target="tpu_custom_call" | custom-call | tf_op jit(solution)/shard_map/solve/pallas_call | solution.py:194
  (10 shorter events, 0.0 us)
Async XLA Ops:
  0.6 2.3 %copy-start = (bf16[16,4096]{1,0:T(8,128)(2,1)S(1)}, bf16[16,4096]{1,0:T(8,128)(2,1)}, u32[]{:S(2)}) copy-start(bf16[16,4096]{1,0:T(8,128)(2,1)} %param.6) | copy-start | bytes 393220
  0.6 0.8 copy-start.1
  1.4 0.8 copy-start.2
  2.2 0.7 copy-start.3
  26.7 18.9 %all-to-all-start = ((f32[16,8,512]{2,1,0:T(8,128)}), f32[16,8,512]{2,1,0:T(8,128)S(1)}, u32[]{:S(2)}, u32[]{:S(2)}) async-start(f32[16,8,512]{2,1,0:T(8,128)} %bitcast.10), calls=%async_computation | async-start | bytes 524288 | tf_op jit(solution)/shard_map/all_to_all | solution.py:33
  46.3 15.1 %all-to-all-start.1 = ((f32[8,8,512]{2,1,0:T(8,128)}), f32[8,8,512]{2,1,0:T(8,128)S(1)}, u32[]{:S(2)}, u32[]{:S(2)}) async-start(f32[8,8,512]{2,1,0:T(8,128)} %reduced.1), calls=%async_computation.1 | async-start | bytes 262144 | tf_op jit(solution)/shard_map/all_to_all | solution.py:33
  62.1 13.1 %all-to-all-start.2 = ((bf16[16,8,512]{2,1,0:T(8,128)(2,1)}), bf16[16,8,512]{2,1,0:T(8,128)(2,1)S(1)}, u32[]{:S(2)}, u32[]{:S(2)}) async-start(bf16[16,8,512]{2,1,0:T(8,128)(2,1)} %weighed.1), calls=%async_computation.2 | async-start | bytes 262144 | tf_op jit(solution)/shard_map/all_to_all | solution.py:33
  86.7 4.7 %copy-start.4 = (bf16[512,4096]{1,0:T(8,128)(2,1)S(1)}, bf16[512,4096]{1,0:T(8,128)(2,1)}, u32[]{:S(2)}) copy-start(bf16[512,4096]{1,0:T(8,128)(2,1)} %fusion.7) | copy-start | bytes 12582916
  86.7 5.9 %copy-start.5 = (bf16[512,4096]{1,0:T(8,128)(2,1)S(1)}, bf16[512,4096]{1,0:T(8,128)(2,1)}, u32[]{:S(2)}) copy-start(bf16[512,4096]{1,0:T(8,128)(2,1)} %fusion.8) | copy-start | bytes 12582916
  93.9 14.0 %all-to-all-start.3 = ((f32[4,16,1024]{2,1,0:T(8,128)}), f32[4,16,1024]{2,1,0:T(8,128)S(1)}, u32[]{:S(2)}, u32[]{:S(2)}) async-start(f32[4,16,1024]{2,1,0:T(8,128)} %bitcast.43), calls=%async_computation.3 | async-start | bytes 524288 | tf_op jit(solution)/shard_map/all_to_all | solution.py:33

commit v5 on v4

--- a/solution.py
+++ b/solution.py
@@ -17,7 +17,7 @@
 NEAR = ("yl", "c", "yh")
 FAR = ("z", "x")
 SPAN = 1024
-FILLS = (1024, 512, 512)
+FILL = 512
 VMEM = pl.BlockSpec(memory_space=pltpu.VMEM)
 
 
@@ -57,6 +57,44 @@
         lanes = slice(i * 128, (i + 1) * 128)
         st_east_ref[i : i + 1, :] = station_ref[0:1, lanes].astype(jnp.float32) * SUBSTEP
         st_north_ref[i : i + 1, :] = station_ref[1:2, lanes].astype(jnp.float32) * SUBSTEP
+
+
+def kept_kernel(first, east_ref, north_ref, squared_ref, scaled_ref, st_east_ref, st_north_ref, sens_ref, se_ref, sn_ref):
+    tile = first // 128 + pl.program_id(0)
+    se_ref[...] = jnp.broadcast_to(st_east_ref[pl.ds(tile, 1), :], (128, 128)).T
+    sn_ref[...] = jnp.broadcast_to(st_north_ref[pl.ds(tile, 1), :], (128, 128)).T
+
+    def span(g, carry):
+        for t in range(2 * SPAN // 128):
+            lanes = pl.ds(pl.multiple_of(g * 2 * SPAN + t * 128, 128), 128)
+            cell_rows = (east_ref, north_ref, squared_ref, scaled_ref)
+            ce, cn, dd, td = [jnp.broadcast_to(ref[0:1, lanes], (16, 128)) for ref in cell_rows]
+            for r in range(8):
+                subs = slice(r * 16, (r + 1) * 16)
+                d_east = ce - se_ref[subs, :]
+                d_north = cn - sn_ref[subs, :]
+                inverse = lax.rsqrt(d_east * d_east + d_north * d_north + dd)
+                sens_ref[subs, lanes] = (td * inverse * inverse * inverse).astype(jnp.bfloat16)
+        return carry
+
+    lax.fori_loop(0, sens_ref.shape[1] // (2 * SPAN), span, 0)
+
+
+def kept(first, geometry):
+    cells = geometry[0].shape[1]
+    return pl.pallas_call(
+        functools.partial(kept_kernel, first),
+        grid=(FILL // 128,),
+        out_shape=pltpu.HBM((FILL, cells), jnp.bfloat16),
+        in_specs=[VMEM] * 6,
+        out_specs=pl.BlockSpec((128, cells), lambda b: (b, 0)),
+        scratch_shapes=[pltpu.VMEM((128, 128), jnp.float32), pltpu.VMEM((128, 128), jnp.float32)],
+        cost_estimate=pl.CostEstimate(
+            flops=10 * FILL * cells, transcendentals=FILL * cells, bytes_accessed=2 * FILL * cells
+        ),
+        compiler_params=pltpu.CompilerParams(vmem_limit_bytes=8 << 20),
+        name="kept",
+    )(*geometry)
 
 
 def sum_of(ref):
@@ -130,7 +168,7 @@
     row = jax.ShapeDtypeStruct((1, cells), f32)
     tiles = jax.ShapeDtypeStruct((stations // 128, 128), f32)
     sources = (cell_plan, cell_depth.reshape(-1, 128), station_index)
-    *cell_geom, st_east, st_north = pl.pallas_call(
+    *cell_geom, tiles_east, tiles_north = pl.pallas_call(
         geometry_kernel,
         grid=(1,),
         out_shape=(row, row, row, row, tiles, tiles),
@@ -139,44 +177,39 @@
         compiler_params=pltpu.CompilerParams(vmem_limit_bytes=8 << 20),
         name="geometry",
     )(*sources)
-    st_east, st_north = st_east.reshape(stations), st_north.reshape(stations)
+    st_east, st_north = tiles_east.reshape(stations), tiles_north.reshape(stations)
     terms = lax.dot_general(
         probes,
         sensitivity(st_east, st_north, cell_geom),
         (((1,), (1,)), ((), ())),
         preferred_element_type=f32,
     )
-    ends = [sum(FILLS[: i + 1]) for i in range(len(FILLS))]
-
-    def kept(i, geometry):
-        here = slice(ends[i] - FILLS[i], ends[i])
-        st_east, st_north, *cell_geom = geometry
-        return sensitivity(st_east[here], st_north[here], cell_geom)
-
-    geometry = (st_east, st_north, *cell_geom)
+    geometry = (*cell_geom, tiles_east, tiles_north)
     blocks = lax.axis_size(SCATTER)
     across = blocks // 2
     width = stations // across
     field = terms.reshape(2, 8, across, width).transpose(0, 2, 1, 3).reshape(blocks, 8, width)
     field, geometry = lax.optimization_barrier((field, geometry))
-    parts, first = lax.optimization_barrier((exchanged(field, SCATTER), kept(0, geometry)))
+    pieces = [kept(0, geometry), kept(FILL, geometry)]
+    parts, pieces = lax.optimization_barrier((exchanged(field, SCATTER), pieces))
     count = lax.axis_size(REDUCE)
     parts = called(copies_kernel, "reduced", jax.ShapeDtypeStruct((count, 8, width), f32), 1)(parts)
     parts, geometry = lax.optimization_barrier((parts, geometry))
-    parts, second = lax.optimization_barrier((exchanged(parts, REDUCE), kept(1, geometry)))
+    parts, piece = lax.optimization_barrier((exchanged(parts, REDUCE), kept(2 * FILL, geometry)))
+    pieces.append(piece)
     start = (lax.axis_index(SCATTER) % across) * width
     own_weight = lax.dynamic_slice_in_dim(station_weight, start, width).reshape(1, width)
     own = called(weigh_kernel, "weighed", jax.ShapeDtypeStruct((blocks, 8, width), jnp.bfloat16), 2)(parts, own_weight)
     own, geometry = lax.optimization_barrier((own, geometry))
-    gathered, third = lax.optimization_barrier((exchanged(own, SCATTER), kept(2, geometry)))
+    gathered, piece = lax.optimization_barrier((exchanged(own, SCATTER), kept(3 * FILL, geometry)))
+    pieces.append(piece)
     weighted = gathered.reshape(2, across, 8, width).transpose(0, 2, 1, 3).reshape(K, stations)
-    backward = jnp.dot(
-        weighted[:, ends[-1] :],
-        sensitivity(geometry[0][ends[-1] :], geometry[1][ends[-1] :], geometry[2:]),
-        preferred_element_type=f32,
-    )
-    for i, sens in enumerate((first, second, third)):
-        segment = weighted[:, ends[i] - FILLS[i] : ends[i]]
+    done = len(pieces) * FILL
+    *cell_geom, tiles_east, tiles_north = geometry
+    st_east, st_north = tiles_east.reshape(stations)[done:], tiles_north.reshape(stations)[done:]
+    backward = jnp.dot(weighted[:, done:], sensitivity(st_east, st_north, cell_geom), preferred_element_type=f32)
+    for i, sens in enumerate(pieces):
+        segment = weighted[:, i * FILL : (i + 1) * FILL]
         backward = backward + jnp.dot(segment, sens, preferred_element_type=f32)
     parts = exchanged(backward.reshape(K, cells // SPAN, SPAN).transpose(1, 0, 2), "yh")
     offset = lax.axis_index("yh") * SPAN

time: 137 us -> 140 us (1.022)
  Pallas kernels: 4.24 us -> 25 us
  other arithmetic: 16.7 us -> 0 us
  matrix products: 41.3 us -> 38.1 us
  local copies, waits for them, and re-layouts: 4.92 us -> 7.13 us
  blocking collectives: 25.8 us -> 28 us
  waiting for transfers between devices: 13 us -> 10.9 us
    pallas_call x0 -> x4, Pallas kernels: none -> 20.7 us  [kept(): pl.pallas_call(functools.partial(kept_kernel, first), grid=(FILL // 128,)...]
    convert_element_type x3 -> x0, other arithmetic: 16.7 us -> none  [sensitivity(): return (down_scaled * inverse * inverse * inverse).astype(jnp.bfloat16)]
    dot_general x3 -> x4, matrix products: 6.06 us -> 2.85 us  [body(): backward = backward + jnp.dot(segment, sens, preferred_element_type=f32)]
    unnamed x12 -> x16, local copies, waits for them, and re-layouts: 2.72 us -> 4.95 us
    all_to_all x2, blocking collectives: 25.8 us -> 28 us  [exchanged(): return lax.all_to_all(blocks, axes, 0, 0, tiled=True)]
    all_to_all x4, waiting for transfers between devices: 13 us -> 10.9 us  [exchanged(): return lax.all_to_all(blocks, axes, 0, 0, tiled=True)]
  transfers between devices with their start and end apart: 4 -> 4, of which waited for: 3 -> 3; matrix products, arithmetic and copies ran while one was open for 13% -> 1% of each run, Pallas kernels for 0% -> 15%
where the time goes in v5:
time: 140 us
  matrix products  38.1 us (27%)
  starting transfers between devices  29.9 us (21%)
  blocking collectives  28 us (20%)
  Pallas kernels  25 us (18%)
  waiting for transfers between devices  10.9 us (8%)
  local copies, waits for them, and re-layouts  7.13 us (5%)
    all_to_all x4, starting transfers between devices, exchanged(): return lax.all_to_all(blocks, axes, 0, 0, tiled=True)  29.9 us
    all_to_all x2, blocking collectives, exchanged(): return lax.all_to_all(blocks, axes, 0, 0, tiled=True)  28 us
    dot_general x1, matrix products, body(): lax.dot_general(probes, sensitivity(st_east, st_north, cell_geom), (((1,)...  23.8 us
    pallas_call x4, Pallas kernels, kept(): pl.pallas_call(functools.partial(kept_kernel, first), grid=(FILL // 128,)...  20.7 us
    dot_general x1, matrix products, body(): jnp.dot(weighted[:, done:], sensitivity(st_east, st_north, cell_geom), pr...  11.5 us
    all_to_all x4, waiting for transfers between devices, exchanged(): return lax.all_to_all(blocks, axes, 0, 0, tiled=True)  10.9 us
    unnamed x16, local copies, waits for them, and re-layouts  4.95 us
    dot_general x4, matrix products, body(): backward = backward + jnp.dot(segment, sens, preferred_element_type=f32)  2.85 us
  transfers between devices with their start and end apart: 4, of which 3 were waited for; matrix products, arithmetic and copies ran while one was open for 1% of the time, Pallas kernels for 15%

profile of v5, /device:TPU:1, one launch (start us, length us, event | category | flops | bytes accessed | tf_op | source)
XLA Modules:
  0.0 139.7 jit_solution(5637071638181629398)
XLA Ops:
  0.6 0.0 copy-start
  0.6 0.0 copy-start.1
  0.7 0.8 copy-done.1
  1.4 0.0 copy-start.2
  1.4 0.8 copy-done.2
  2.2 0.0 copy-start.3
  2.2 0.7 copy-done.3
  2.9 0.1 geometry.1
  3.0 0.0 copy-done
  3.0 23.8 %fusion.2 = f32[4096,16]{0,1:T(8,128)} fusion(bf16[16,4096]{1,0:T(8,128)(2,1)S(1)} %copy-done, f32[4096]{0:T(1024)S(1)} %bitcast.47, f32[4096]{0:T(1024)S(1)} %bitcast.42, f32[4096]{0:T(1024)S(1)} %bitcast.45, f32[4096]{0:T(1024)S(1)} %bitcast.41, f32[4096]{0:T(1024)S(1)} %bitcast.43, f32[4096]{0:T(1024)S(1)} %bitcast.49), kind=kOutput, calls=%fused_computation.4 | convolution fusion | flops 704643072 | bytes 491520 | tf_op jit(solution)/shard_map/dot_general | solution.py:181
  26.7 10.4 %all-to-all-start = ((f32[16,8,512]{2,1,0:T(8,128)}), f32[16,8,512]{2,1,0:T(8,128)S(1)}, u32[]{:S(2)}, u32[]{:S(2)}) async-start(f32[16,8,512]{2,1,0:T(8,128)} %bitcast.10), calls=%async_computation | async-start | bytes 524288 | tf_op jit(solution)/shard_map/all_to_all | solution.py:33
  37.1 5.2 %kept.5 = bf16[512,4096]{1,0:T(8,128)(2,1)} custom-call(f32[1,4096]{1,0:T(1,128)S(1)} %get-tuple-element.61.east_ref, f32[1,4096]{1,0:T(1,128)S(1)} %get-tuple-element.62.north_ref, f32[1,4096]{1,0:T(1,128)S(1)} %get-tuple-element.63.squared_ref, f32[1,4096]{1,0:T(1,128)S(1)} %get-tuple-element.64.scaled_ref, f32[32,128]{1,0:T(8,128)S(1)} %get-tuple-element.65.st_east_ref, ...), custom_call_target="tpu_custom_call" | custom-call | flops 20971520 | bytes 4194304 | tf_op jit(solution)/shard_map/kept/pallas_call | solution.py:85
  42.3 5.2 %kept.4 = bf16[512,4096]{1,0:T(8,128)(2,1)} custom-call(f32[1,4096]{1,0:T(1,128)S(1)} %get-tuple-element.61.east_ref, f32[1,4096]{1,0:T(1,128)S(1)} %get-tuple-element.62.north_ref, f32[1,4096]{1,0:T(1,128)S(1)} %get-tuple-element.63.squared_ref, f32[1,4096]{1,0:T(1,128)S(1)} %get-tuple-element.64.scaled_ref, f32[32,128]{1,0:T(8,128)S(1)} %get-tuple-element.65.st_east_ref, ...), custom_call_target="tpu_custom_call" | custom-call | flops 20971520 | bytes 4194304 | tf_op jit(solution)/shard_map/kept/pallas_call | solution.py:85
  47.5 0.0 all-to-all-done.parts_ref
  47.5 0.7 reduced.1
  48.2 6.7 %all-to-all-start.1 = ((f32[8,8,512]{2,1,0:T(8,128)}), f32[8,8,512]{2,1,0:T(8,128)S(1)}, u32[]{:S(2)}, u32[]{:S(2)}) async-start(f32[8,8,512]{2,1,0:T(8,128)} %reduced.1), calls=%async_computation.1 | async-start | bytes 262144 | tf_op jit(solution)/shard_map/all_to_all | solution.py:33
  54.9 0.8 dynamic_slice.9
  55.6 5.2 %kept.6 = bf16[512,4096]{1,0:T(8,128)(2,1)} custom-call(f32[1,4096]{1,0:T(1,128)S(1)} %get-tuple-element.61.east_ref, f32[1,4096]{1,0:T(1,128)S(1)} %get-tuple-element.62.north_ref, f32[1,4096]{1,0:T(1,128)S(1)} %get-tuple-element.63.squared_ref, f32[1,4096]{1,0:T(1,128)S(1)} %get-tuple-element.64.scaled_ref, f32[32,128]{1,0:T(8,128)S(1)} %get-tuple-element.65.st_east_ref, ...), custom_call_target="tpu_custom_call" | custom-call | flops 20971520 | bytes 4194304 | tf_op jit(solution)/shard_map/kept/pallas_call | solution.py:85
  60.8 2.5 %all-to-all-done.1.parts_ref = f32[8,8,512]{2,1,0:T(8,128)S(1)} async-done(((f32[8,8,512]{2,1,0:T(8,128)}), f32[8,8,512]{2,1,0:T(8,128)S(1)}, u32[]{:S(2)}, u32[]{:S(2)}) %all-to-all-start.1) | async-done | bytes 131104 | tf_op jit(solution)/shard_map/all_to_all | solution.py:33
  63.3 0.7 weighed.1
  64.0 6.9 %all-to-all-start.2 = ((bf16[16,8,512]{2,1,0:T(8,128)(2,1)}), bf16[16,8,512]{2,1,0:T(8,128)(2,1)S(1)}, u32[]{:S(2)}, u32[]{:S(2)}) async-start(bf16[16,8,512]{2,1,0:T(8,128)(2,1)} %weighed.1), calls=%async_computation.2 | async-start | bytes 262144 | tf_op jit(solution)/shard_map/all_to_all | solution.py:33
  70.9 5.2 %kept.7 = bf16[512,4096]{1,0:T(8,128)(2,1)} custom-call(f32[1,4096]{1,0:T(1,128)S(1)} %get-tuple-element.61.east_ref, f32[1,4096]{1,0:T(1,128)S(1)} %get-tuple-element.62.north_ref, f32[1,4096]{1,0:T(1,128)S(1)} %get-tuple-element.63.squared_ref, f32[1,4096]{1,0:T(1,128)S(1)} %get-tuple-element.64.scaled_ref, f32[32,128]{1,0:T(8,128)S(1)} %get-tuple-element.65.st_east_ref, ...), custom_call_target="tpu_custom_call" | custom-call | flops 20971520 | bytes 4194304 | tf_op jit(solution)/shard_map/kept/pallas_call | solution.py:85
  76.1 1.0 all-to-all-done.2
  77.1 0.0 copy-start.5
  77.1 11.5 %fusion.4 = f32[16,4096]{1,0:T(8,128)S(1)} fusion(f32[4096]{0:T(1024)S(1)} %bitcast.48, f32[2048]{0:T(1024)S(1)} %get-tuple-element.74, f32[4096]{0:T(1024)S(1)} %bitcast.46, f32[2048]{0:T(1024)S(1)} %get-tuple-element.75, f32[4096]{0:T(1024)S(1)} %bitcast.44, f32[4096]{0:T(1024)S(1)} %bitcast.50, bf16[16,4096]{1,0:T(8,128)(2,1)S(1)} %bitcast.55), kind=kOutput, calls=%fused_computation.5 | convolution fusion | flops 352321536 | bytes 409600 | tf_op jit(solution)/shard_map/dot_general | solution.py:210
  88.6 0.0 copy-done.5
  88.6 0.0 copy-start.4
  88.6 0.0 copy-start.6
  88.6 0.9 convolution_add_fusion.3
  89.5 1.3 copy-done.4
  90.8 0.0 copy-start.7
  90.8 0.7 convolution_add_fusion.2
  91.4 0.6 copy-done.6
  92.1 0.7 convolution_add_fusion.1
  92.7 0.7 copy-done.7
  93.5 0.7 convolution_add_fusion
  94.1 0.7 copy.11
  94.9 5.9 %all-to-all-start.3 = ((f32[4,16,1024]{2,1,0:T(8,128)}), f32[4,16,1024]{2,1,0:T(8,128)S(1)}, u32[]{:S(2)}, u32[]{:S(2)}) async-start(f32[4,16,1024]{2,1,0:T(8,128)} %bitcast.40), calls=%async_computation.3 | async-start | bytes 524288 | tf_op jit(solution)/shard_map/all_to_all | solution.py:33
  100.8 0.7 dynamic_slice.10
  101.5 7.4 %all-to-all-done.3.parts_ref = f32[4,16,1024]{2,1,0:T(8,128)S(1)} async-done(((f32[4,16,1024]{2,1,0:T(8,128)}), f32[4,16,1024]{2,1,0:T(8,128)S(1)}, u32[]{:S(2)}, u32[]{:S(2)}) %all-to-all-start.3) | async-done | bytes 262176 | tf_op jit(solution)/shard_map/all_to_all | solution.py:33
  108.8 0.5 gram.1
  109.4 13.8 %all_to_all.30.parts_ref = f32[16,2,128]{2,1,0:T(2,128)S(1)} all-to-all(f32[16,2,128]{2,1,0:T(2,128)S(1)} %get-tuple-element.72), channel_id=1, replica_groups=mesh['z'=8,'yl'=2,'x'=4,'c'=2,'yh'=4] {'yl','c','yh'}, dimensions={0} | all-to-all | bytes 32768 | tf_op jit(solution)/shard_map/all_to_all | solution.py:33
  123.2 14.2 %all_to_all.31.parts_ref = f32[32,2,128]{2,1,0:T(2,128)S(1)} all-to-all(f32[32,2,128]{2,1,0:T(2,128)S(1)} %summed.1), channel_id=1, replica_groups=mesh['z'=8,'yl'=2,'x'=4,'c'=2,'yh'=4] {'z','x'}, dimensions={0} | all-to-all | bytes 65536 | tf_op jit(solution)/shard_map/all_to_all | solution.py:33
  137.4 2.3 %solve.1 = (f32[16,1024]{1,0:T(8,128)}, f32[16,16]{1,0:T(8,128)}) custom-call(f32[32,2,128]{2,1,0:T(2,128)S(1)} %all_to_all.31.parts_ref, f32[16,1024]{1,0:T(8,128)S(1)} %get-tuple-element.73.image_ref), custom_call_target="tpu_custom_call" | custom-call | tf_op jit(solution)/shard_map/solve/pallas_call | solution.py:227
  (3 shorter events, 0.0 us)
Async XLA Ops:
  0.6 2.3 %copy-start = (bf16[16,4096]{1,0:T(8,128)(2,1)S(1)}, bf16[16,4096]{1,0:T(8,128)(2,1)}, u32[]{:S(2)}) copy-start(bf16[16,4096]{1,0:T(8,128)(2,1)} %param.6) | copy-start | bytes 393220
  0.6 0.8 copy-start.1
  1.4 0.8 copy-start.2
  2.2 0.7 copy-start.3
  26.7 20.8 %all-to-all-start = ((f32[16,8,512]{2,1,0:T(8,128)}), f32[16,8,512]{2,1,0:T(8,128)S(1)}, u32[]{:S(2)}, u32[]{:S(2)}) async-start(f32[16,8,512]{2,1,0:T(8,128)} %bitcast.10), calls=%async_computation | async-start | bytes 524288 | tf_op jit(solution)/shard_map/all_to_all | solution.py:33
  48.2 15.1 %all-to-all-start.1 = ((f32[8,8,512]{2,1,0:T(8,128)}), f32[8,8,512]{2,1,0:T(8,128)S(1)}, u32[]{:S(2)}, u32[]{:S(2)}) async-start(f32[8,8,512]{2,1,0:T(8,128)} %reduced.1), calls=%async_computation.1 | async-start | bytes 262144 | tf_op jit(solution)/shard_map/all_to_all | solution.py:33
  64.0 13.1 %all-to-all-start.2 = ((bf16[16,8,512]{2,1,0:T(8,128)(2,1)}), bf16[16,8,512]{2,1,0:T(8,128)(2,1)S(1)}, u32[]{:S(2)}, u32[]{:S(2)}) async-start(bf16[16,8,512]{2,1,0:T(8,128)(2,1)} %weighed.1), calls=%async_computation.2 | async-start | bytes 262144 | tf_op jit(solution)/shard_map/all_to_all | solution.py:33
  77.1 11.5 %copy-start.5 = (bf16[512,4096]{1,0:T(8,128)(2,1)S(1)}, bf16[512,4096]{1,0:T(8,128)(2,1)}, u32[]{:S(2)}) copy-start(bf16[512,4096]{1,0:T(8,128)(2,1)} %kept.4) | copy-start | bytes 12582916
  88.6 2.2 %copy-start.4 = (bf16[512,4096]{1,0:T(8,128)(2,1)S(1)}, bf16[512,4096]{1,0:T(8,128)(2,1)}, u32[]{:S(2)}) copy-start(bf16[512,4096]{1,0:T(8,128)(2,1)} %kept.5) | copy-start | bytes 12582916
  88.6 3.5 %copy-start.6 = (bf16[512,4096]{1,0:T(8,128)(2,1)S(1)}, bf16[512,4096]{1,0:T(8,128)(2,1)}, u32[]{:S(2)}) copy-start(bf16[512,4096]{1,0:T(8,128)(2,1)} %kept.6) | copy-start | bytes 12582916
  90.8 2.7 %copy-start.7 = (bf16[512,4096]{1,0:T(8,128)(2,1)S(1)}, bf16[512,4096]{1,0:T(8,128)(2,1)}, u32[]{:S(2)}) copy-start(bf16[512,4096]{1,0:T(8,128)(2,1)} %kept.7) | copy-start | bytes 12582916
  94.9 14.0 %all-to-all-start.3 = ((f32[4,16,1024]{2,1,0:T(8,128)}), f32[4,16,1024]{2,1,0:T(8,128)S(1)}, u32[]{:S(2)}, u32[]{:S(2)}) async-start(f32[4,16,1024]{2,1,0:T(8,128)} %bitcast.40), calls=%async_computation.3 | async-start | bytes 524288 | tf_op jit(solution)/shard_map/all_to_all | solution.py:33

commit v6 on v4

--- a/solution.py
+++ b/solution.py
@@ -17,7 +17,7 @@
 NEAR = ("yl", "c", "yh")
 FAR = ("z", "x")
 SPAN = 1024
-FILLS = (1024, 512, 512)
+FILLS = (768, 512, 512)
 VMEM = pl.BlockSpec(memory_space=pltpu.VMEM)
 
 

time: 137 us -> 135 us (0.985)
  matrix products: 41.3 us -> 39.1 us
  local copies, waits for them, and re-layouts: 4.92 us -> 6.33 us
  other arithmetic: 16.7 us -> 15.3 us
    dot_general x3, matrix products: 6.06 us -> 2.25 us  [body(): backward = backward + jnp.dot(segment, sens, preferred_element_type=f32)]
    dot_general x1, matrix products: 11.5 us -> 13.1 us  [body(): jnp.dot(weighted[:, ends[-1]:], sensitivity(geometry[0][ends[-1]:], geome...]
    convert_element_type x3, other arithmetic: 16.7 us -> 15.3 us  [sensitivity(): return (down_scaled * inverse * inverse * inverse).astype(jnp.bfloat16)]
    unnamed x12 -> x16, local copies, waits for them, and re-layouts: 2.72 us -> 4.14 us
  transfers between devices with their start and end apart: 4 -> 4, of which waited for: 3 -> 4; matrix products, arithmetic and copies ran while one was open for 13% -> 12% of each run, Pallas kernels for 0% -> 0%
where the time goes in v6:
time: 135 us; the launch traced here: 134 us
  matrix products  39.1 us (29%)
  starting transfers between devices  30 us (22%)
  blocking collectives  26 us (19%)
  other arithmetic  15.3 us (11%)
  waiting for transfers between devices  12.7 us (9%)
  local copies, waits for them, and re-layouts  6.33 us (5%)
  Pallas kernels  4.24 us (3%)
    all_to_all x4, starting transfers between devices, exchanged(): return lax.all_to_all(blocks, axes, 0, 0, tiled=True)  30 us
    all_to_all x2, blocking collectives, exchanged(): return lax.all_to_all(blocks, axes, 0, 0, tiled=True)  26 us
    dot_general x1, matrix products, body(): lax.dot_general(probes, sensitivity(st_east, st_north, cell_geom), (((1,)...  23.7 us
    convert_element_type x3, other arithmetic, sensitivity(): return (down_scaled * inverse * inverse * inverse).astype(jnp.bfloat16)  15.3 us
    dot_general x1, matrix products, body(): jnp.dot(weighted[:, ends[-1]:], sensitivity(geometry[0][ends[-1]:], geome...  13.1 us
    all_to_all x4, waiting for transfers between devices, exchanged(): return lax.all_to_all(blocks, axes, 0, 0, tiled=True)  12.7 us
    unnamed x16, local copies, waits for them, and re-layouts  4.14 us
  transfers between devices with their start and end apart: 4, of which 4 were waited for; matrix products, arithmetic and copies ran while one was open for 12% of the time, Pallas kernels for 0%

profile of v6, /device:TPU:1, one launch (start us, length us, event | category | flops | bytes accessed | tf_op | source)
XLA Modules:
  0.0 134.4 jit_solution(17181384380696896659)
XLA Ops:
  0.6 0.0 copy-start
  0.6 0.0 copy-start.1
  0.7 0.8 copy-done.1
  1.4 0.0 copy-start.2
  1.4 0.8 copy-done.2
  2.2 0.0 copy-start.3
  2.2 0.7 copy-done.3
  2.9 0.1 geometry.1
  3.0 0.0 copy-done
  3.0 23.7 %fusion.2 = f32[4096,16]{0,1:T(8,128)} fusion(bf16[16,4096]{1,0:T(8,128)(2,1)S(1)} %copy-done, f32[4096]{0:T(1024)S(1)} %bitcast.54, f32[4096]{0:T(1024)S(1)} %bitcast.64, f32[4096]{0:T(1024)S(1)} %bitcast.49, f32[4096]{0:T(1024)S(1)} %bitcast.69, f32[4096]{0:T(1024)S(1)} %bitcast.44, f32[4096]{0:T(1024)S(1)} %bitcast.59), kind=kOutput, calls=%fused_computation.4 | convolution fusion | flops 704643072 | bytes 491520 | tf_op jit(solution)/shard_map/dot_general | solution.py:143
  26.7 10.4 %all-to-all-start = ((f32[16,8,512]{2,1,0:T(8,128)}), f32[16,8,512]{2,1,0:T(8,128)S(1)}, u32[]{:S(2)}, u32[]{:S(2)}) async-start(f32[16,8,512]{2,1,0:T(8,128)} %bitcast.10), calls=%async_computation | async-start | bytes 524288 | tf_op jit(solution)/shard_map/all_to_all | solution.py:33
  37.1 6.1 %fusion.6 = bf16[768,4096]{1,0:T(8,128)(2,1)} fusion(f32[4096]{0:T(1024)S(1)} %bitcast.55, f32[768]{0:T(1024)S(1)} %slice.37, f32[4096]{0:T(1024)S(1)} %bitcast.50, f32[768]{0:T(1024)S(1)} %slice.36, f32[4096]{0:T(1024)S(1)} %bitcast.45, f32[4096]{0:T(1024)S(1)} %bitcast.60), kind=kLoop, calls=%fused_computation.7 | loop fusion | flops 31457280 | bytes 6363136 | tf_op jit(solution)/shard_map/convert_element_type | solution.py:29
  43.3 0.8 dynamic_slice.9
  44.0 0.3 all-to-all-done.parts_ref
  44.3 0.7 reduced.1
  45.0 6.6 %all-to-all-start.1 = ((f32[8,8,512]{2,1,0:T(8,128)}), f32[8,8,512]{2,1,0:T(8,128)S(1)}, u32[]{:S(2)}, u32[]{:S(2)}) async-start(f32[8,8,512]{2,1,0:T(8,128)} %reduced.1), calls=%async_computation.1 | async-start | bytes 262144 | tf_op jit(solution)/shard_map/all_to_all | solution.py:33
  51.6 4.6 %fusion.7 = bf16[512,4096]{1,0:T(8,128)(2,1)} fusion(f32[4096]{0:T(1024)S(1)} %bitcast.56, f32[512]{0:T(512)S(1)} %slice.39, f32[4096]{0:T(1024)S(1)} %bitcast.51, f32[512]{0:T(512)S(1)} %slice.38, f32[4096]{0:T(1024)S(1)} %bitcast.46, f32[4096]{0:T(1024)S(1)} %bitcast.61), kind=kLoop, calls=%fused_computation.10 | loop fusion | flops 20971520 | bytes 4263936 | tf_op jit(solution)/shard_map/convert_element_type | solution.py:29
  56.2 3.5 %all-to-all-done.1.parts_ref = f32[8,8,512]{2,1,0:T(8,128)S(1)} async-done(((f32[8,8,512]{2,1,0:T(8,128)}), f32[8,8,512]{2,1,0:T(8,128)S(1)}, u32[]{:S(2)}, u32[]{:S(2)}) %all-to-all-start.1) | async-done | bytes 131104 | tf_op jit(solution)/shard_map/all_to_all | solution.py:33
  59.6 0.7 weighed.1
  60.3 7.1 %all-to-all-start.2 = ((bf16[16,8,512]{2,1,0:T(8,128)(2,1)}), bf16[16,8,512]{2,1,0:T(8,128)(2,1)S(1)}, u32[]{:S(2)}, u32[]{:S(2)}) async-start(bf16[16,8,512]{2,1,0:T(8,128)(2,1)} %weighed.1), calls=%async_computation.2 | async-start | bytes 262144 | tf_op jit(solution)/shard_map/all_to_all | solution.py:33
  67.4 0.0 slice-start
  67.4 4.6 %fusion.8 = bf16[512,4096]{1,0:T(8,128)(2,1)} fusion(f32[4096]{0:T(1024)S(1)} %bitcast.57, f32[512]{0:T(512)S(1)} %slice.41, f32[4096]{0:T(1024)S(1)} %bitcast.52, f32[512]{0:T(512)S(1)} %slice.40, f32[4096]{0:T(1024)S(1)} %bitcast.47, f32[4096]{0:T(1024)S(1)} %bitcast.62), kind=kLoop, calls=%fused_computation.11 | loop fusion | flops 20971520 | bytes 4263936 | tf_op jit(solution)/shard_map/convert_element_type | solution.py:29
  72.0 1.6 %all-to-all-done.2 = bf16[16,8,512]{2,1,0:T(8,128)(2,1)S(1)} async-done(((bf16[16,8,512]{2,1,0:T(8,128)(2,1)}), bf16[16,8,512]{2,1,0:T(8,128)(2,1)S(1)}, u32[]{:S(2)}, u32[]{:S(2)}) %all-to-all-start.2) | async-done | bytes 131104 | tf_op jit(solution)/shard_map/all_to_all | solution.py:33
  73.6 0.0 slice-start.1
  73.6 13.1 %fusion.4 = f32[16,4096]{1,0:T(8,128)S(1)} fusion(f32[4096]{0:T(1024)S(1)} %bitcast.58, f32[2304]{0:T(1024)S(1)} %slice.44, f32[4096]{0:T(1024)S(1)} %bitcast.53, f32[2304]{0:T(1024)S(1)} %slice.43, f32[4096]{0:T(1024)S(1)} %bitcast.48, f32[4096]{0:T(1024)S(1)} %bitcast.63, bf16[16,4096]{1,0:T(8,128)(2,1)S(1)} %bitcast.80), kind=kOutput, calls=%fused_computation.6 | convolution fusion | flops 396361728 | bytes 425984 | tf_op jit(solution)/shard_map/dot_general | solution.py:173
  86.7 0.0 slice-done
  86.7 0.0 slice-done.1
  86.7 0.0 copy-start.4
  86.8 0.0 copy-start.5
  86.8 0.9 convolution_add_fusion.2
  87.7 1.2 copy-done.4
  88.9 0.7 convolution_add_fusion.1
  89.6 0.6 copy-done.5
  90.2 0.7 convolution_add_fusion
  90.9 0.7 copy.11
  91.6 5.9 %all-to-all-start.3 = ((f32[4,16,1024]{2,1,0:T(8,128)}), f32[4,16,1024]{2,1,0:T(8,128)S(1)}, u32[]{:S(2)}, u32[]{:S(2)}) async-start(f32[4,16,1024]{2,1,0:T(8,128)} %bitcast.43), calls=%async_computation.3 | async-start | bytes 524288 | tf_op jit(solution)/shard_map/all_to_all | solution.py:33
  97.5 0.7 dynamic_slice.10
  98.2 7.4 %all-to-all-done.3.parts_ref = f32[4,16,1024]{2,1,0:T(8,128)S(1)} async-done(((f32[4,16,1024]{2,1,0:T(8,128)}), f32[4,16,1024]{2,1,0:T(8,128)S(1)}, u32[]{:S(2)}, u32[]{:S(2)}) %all-to-all-start.3) | async-done | bytes 262176 | tf_op jit(solution)/shard_map/all_to_all | solution.py:33
  105.6 0.5 gram.1
  106.1 13.8 %all_to_all.30.parts_ref = f32[16,2,128]{2,1,0:T(2,128)S(1)} all-to-all(f32[16,2,128]{2,1,0:T(2,128)S(1)} %get-tuple-element.70), channel_id=1, replica_groups=mesh['z'=8,'yl'=2,'x'=4,'c'=2,'yh'=4] {'yl','c','yh'}, dimensions={0} | all-to-all | bytes 32768 | tf_op jit(solution)/shard_map/all_to_all | solution.py:33
  119.9 12.2 %all_to_all.31.parts_ref = f32[32,2,128]{2,1,0:T(2,128)S(1)} all-to-all(f32[32,2,128]{2,1,0:T(2,128)S(1)} %summed.1), channel_id=1, replica_groups=mesh['z'=8,'yl'=2,'x'=4,'c'=2,'yh'=4] {'z','x'}, dimensions={0} | all-to-all | bytes 65536 | tf_op jit(solution)/shard_map/all_to_all | solution.py:33
  132.2 2.3 %solve.1 = (f32[16,1024]{1,0:T(8,128)}, f32[16,16]{1,0:T(8,128)}) custom-call(f32[32,2,128]{2,1,0:T(2,128)S(1)} %all_to_all.31.parts_ref, f32[16,1024]{1,0:T(8,128)S(1)} %get-tuple-element.71.image_ref), custom_call_target="tpu_custom_call" | custom-call | tf_op jit(solution)/shard_map/solve/pallas_call | solution.py:194
  (11 shorter events, 0.1 us)
Async XLA Ops:
  0.6 2.3 %copy-start = (bf16[16,4096]{1,0:T(8,128)(2,1)S(1)}, bf16[16,4096]{1,0:T(8,128)(2,1)}, u32[]{:S(2)}) copy-start(bf16[16,4096]{1,0:T(8,128)(2,1)} %param.6) | copy-start | bytes 393220
  0.6 0.8 copy-start.1
  1.4 0.8 copy-start.2
  2.2 0.7 copy-start.3
  26.7 17.6 %all-to-all-start = ((f32[16,8,512]{2,1,0:T(8,128)}), f32[16,8,512]{2,1,0:T(8,128)S(1)}, u32[]{:S(2)}, u32[]{:S(2)}) async-start(f32[16,8,512]{2,1,0:T(8,128)} %bitcast.10), calls=%async_computation | async-start | bytes 524288 | tf_op jit(solution)/shard_map/all_to_all | solution.py:33
  45.0 14.6 %all-to-all-start.1 = ((f32[8,8,512]{2,1,0:T(8,128)}), f32[8,8,512]{2,1,0:T(8,128)S(1)}, u32[]{:S(2)}, u32[]{:S(2)}) async-start(f32[8,8,512]{2,1,0:T(8,128)} %reduced.1), calls=%async_computation.1 | async-start | bytes 262144 | tf_op jit(solution)/shard_map/all_to_all | solution.py:33
  60.3 13.3 %all-to-all-start.2 = ((bf16[16,8,512]{2,1,0:T(8,128)(2,1)}), bf16[16,8,512]{2,1,0:T(8,128)(2,1)S(1)}, u32[]{:S(2)}, u32[]{:S(2)}) async-start(bf16[16,8,512]{2,1,0:T(8,128)(2,1)} %weighed.1), calls=%async_computation.2 | async-start | bytes 262144 | tf_op jit(solution)/shard_map/all_to_all | solution.py:33
  67.4 19.3 %slice-start = ((s8[6291456]{0:T(1024)(128)(4,1)}), s8[2097152]{0:T(1024)(128)(4,1)S(1)}, s32[]{:S(2)}) async-start(s8[6291456]{0:T(1024)(128)(4,1)} %bitcast.77), calls=%async_computation.6 | async-start | bytes 4194304
  73.6 13.2 %slice-start.1 = ((s8[6291456]{0:T(1024)(128)(4,1)}), s8[4194304]{0:T(1024)(128)(4,1)S(1)}, s32[]{:S(2)}) async-start(s8[6291456]{0:T(1024)(128)(4,1)} %bitcast.77), calls=%async_computation.7 | async-start | bytes 8388608
  86.7 2.2 %copy-start.4 = (bf16[512,4096]{1,0:T(8,128)(2,1)S(1)}, bf16[512,4096]{1,0:T(8,128)(2,1)}, u32[]{:S(2)}) copy-start(bf16[512,4096]{1,0:T(8,128)(2,1)} %fusion.7) | copy-start | bytes 12582916
  86.8 3.5 %copy-start.5 = (bf16[512,4096]{1,0:T(8,128)(2,1)S(1)}, bf16[512,4096]{1,0:T(8,128)(2,1)}, u32[]{:S(2)}) copy-start(bf16[512,4096]{1,0:T(8,128)(2,1)} %fusion.8) | copy-start | bytes 12582916
  91.6 14.0 %all-to-all-start.3 = ((f32[4,16,1024]{2,1,0:T(8,128)}), f32[4,16,1024]{2,1,0:T(8,128)S(1)}, u32[]{:S(2)}, u32[]{:S(2)}) async-start(f32[4,16,1024]{2,1,0:T(8,128)} %bitcast.43), calls=%async_computation.3 | async-start | bytes 524288 | tf_op jit(solution)/shard_map/all_to_all | solution.py:33
